TPU v7x, 128 devices: a whole 4x4x4 slice. The times are simulated.
128 devices in a mesh: seq: 16 (over x, y_hi, core), fsdp: 8 (over z, y_lo).
Axes of the slice: x: 4, y: 4 (y_hi: 2, y_lo: 2; y = y_hi * 2 + y_lo), z: 4, core: 2. Of those that a mesh axis runs over, the one named last changes fastest.
Arguments:
- normed: bfloat16 [131072, 1024], P(('seq', 'fsdp')), may hold values from -31 to 31, as said below
- w_qkv: bfloat16 [1024, 3072], P('fsdp'), may hold values from -0.5 to 0.5, as said below
- w_out: bfloat16 [1024, 1024], P('fsdp'), may hold values from -0.5 to 0.5
- layout: int32 [1024, 10], P(('seq', 'fsdp')), may hold values from 0 to 23, as said below
- counts: int32 [1024], P(('seq', 'fsdp')), may hold values from 1 to 10, as said below
Outputs:
- mixed: bfloat16 [131072, 1024], P(('seq', 'fsdp'))
Inputs may be any that keep to these rules, and one draw needn't show every extreme that they name: `normed`: float activations. `w_qkv`: float weights. `layout`: each row holds 10 distinct pool entries, never the query block's own entry; entries 0 to 7 name the blocks of the station one step lower along seq, the last 8 those one step higher. `counts`: the value 10 occurs in every draw.
All inputs are finite; a program needn't handle non-finite values.
Results may differ from a plain program's by a relative error of at most 0.0099.
Values may be sent and summed in bfloat16 or wider, within the bound.
A program may use at most 128 MiB of HBM per device.

v0:
```python
import math

import jax
import jax.numpy as jnp
from jax import lax
from jax.sharding import PartitionSpec as P

HEADS = 8
BLOCK = 128
KEY_BLOCKS = 10


def from_behind(value, axis, steps):
    count = lax.axis_size(axis)
    pairs = [(source, (source + steps) % count) for source in range(count)]
    return lax.ppermute(value, axis, pairs)


def attend(query, own_blocks, picked, used):
    block_count = picked.shape[0]
    feature_width = query.shape[1]
    head_width = feature_width // HEADS
    keyvals = jnp.concatenate([own_blocks[:, None], picked], axis=1)
    keyvals = keyvals.reshape(block_count, (KEY_BLOCKS + 1) * BLOCK, 2 * feature_width)
    key_heads = keyvals[..., :feature_width].reshape(block_count, -1, HEADS, head_width)
    value_heads = keyvals[..., feature_width:].reshape(block_count, -1, HEADS, head_width)
    query_heads = query.reshape(block_count, BLOCK, HEADS, head_width)
    scores = jnp.einsum(
        "bqhd,bkhd->bhqk", query_heads, key_heads, preferred_element_type=jnp.float32
    )
    scores = scores * head_width ** (-0.5)
    slot_number = jnp.arange((KEY_BLOCKS + 1) * BLOCK, dtype=jnp.int32) // BLOCK
    usable = slot_number[None, :] <= used[:, None]
    scores = jnp.where(usable[:, None, None, :], scores, -jnp.inf)
    largest = jnp.max(scores, axis=-1, keepdims=True)
    expons = jnp.exp(scores - largest)
    denominator = jnp.sum(expons, axis=-1, keepdims=True)
    rounded = expons.astype(jnp.bfloat16)
    summed = jnp.einsum("bhqk,bkhd->bqhd", rounded, value_heads, preferred_element_type=jnp.float32)
    summed = summed / jnp.transpose(denominator, (0, 2, 1, 3))
    return summed.reshape(block_count * BLOCK, feature_width).astype(jnp.bfloat16)


def shards(normed, w_qkv, w_out, layout, counts):
    row_count, feature_width = normed.shape
    blocks_here = row_count // BLOCK
    sources = (normed,)
    start_sums = [jnp.zeros((row_count, 3 * feature_width), jnp.float32)]
    start_sums = tuple(start_sums)
    own_cols = sources[0]
    fresh = [
        jnp.dot(
            own_cols,
            lax.all_gather(w_qkv, "fsdp", axis=0, tiled=True),
            preferred_element_type=jnp.float32,
        )
    ]
    sums = tuple(fresh)
    packed = sums[0].astype(jnp.bfloat16)
    queries = packed[:, :feature_width]
    keyvals = packed[:, feature_width:]
    lower_keys = from_behind(keyvals, "seq", 1)
    upper_keys = from_behind(keyvals, "seq", -1)
    pool_rows = jnp.concatenate([lower_keys, keyvals, upper_keys], axis=0)
    pool = pool_rows.reshape(3 * blocks_here, BLOCK, 2 * feature_width)
    group_size = math.gcd(blocks_here, max(1, 256 // BLOCK))
    group_count = blocks_here // group_size

    def one_group(items):
        query_part, layout_part, count_part, group_number = items
        own_blocks = lax.dynamic_slice_in_dim(
            pool, blocks_here + group_number * group_size, group_size, 0
        )
        picked = pool[layout_part]
        return attend(query_part, own_blocks, picked, count_part)

    attended = lax.map(
        one_group,
        (
            queries.reshape(group_count, group_size * BLOCK, feature_width),
            layout.reshape(group_count, group_size, KEY_BLOCKS),
            counts.reshape(group_count, group_size),
            jnp.arange(group_count, dtype=jnp.int32),
        ),
    )
    attended = attended.reshape(row_count, feature_width)
    output_sum = jnp.dot(
        attended,
        lax.all_gather(w_out, "fsdp", axis=0, tiled=True),
        preferred_element_type=jnp.float32,
    )
    return output_sum.astype(jnp.bfloat16)


def solution(mesh):
    return jax.shard_map(
        shards,
        mesh=mesh,
        in_specs=(
            P(("seq", "fsdp"), None),
            P("fsdp", None),
            P("fsdp", None),
            P(("seq", "fsdp"), None),
            P(("seq", "fsdp")),
        ),
        out_specs=P(("seq", "fsdp"), None),
        check_vma=False,
    )
```

profile of v0, /device:TPU:1, one launch (start us, length us, event | category | flops | bytes accessed | tf_op | source)
XLA Modules:
  0.0 604.0 jit_solution(1905112295235655145)
XLA Ops:
  6.5 0.7 all-gather.3.cloned.1.call-update
  7.3 134.3 %all-gather.3.cloned.1.call-done = bf16[1024,3072]{1,0:T(8,128)(2,1)} async-done(((bf16[128,3072]{1,0:T(8,128)(2,1)}), bf16[1024,3072]{1,0:T(8,128)(2,1)}) %all-gather.3.cloned.1.call-update) | async-done | bytes 6291472 | tf_op jit(solution)/shard_map/all_gather | solution.py:54
  141.6 9.6 %convolution_convert_fusion = bf16[1024,3072]{1,0:T(8,128)(2,1)S(1)} fusion(bf16[1024,1024]{1,0:T(8,128)(2,1)S(1)} %copy-done, bf16[1024,3072]{1,0:T(8,128)(2,1)} %all-gather.3.cloned.1.call-done), kind=kOutput, calls=%fused_computation.36 | convolution fusion | flops 6445596672 | bytes 14680064 | tf_op jit(solution)/shard_map/dot_general | solution.py:52
  151.3 2.7 copy-done.3
  153.9 2.2 slice.24
  156.2 3.2 collective-permute-start
  159.5 3.1 slice.25
  162.6 126.8 %collective-permute-done = bf16[1024,2048]{1,0:T(8,128)(2,1)} collective-permute-done((bf16[1024,2048]{1,0:T(8,128)(2,1)}, bf16[1024,2048]{1,0:T(8,128)(2,1)}, u32[]{:S(2)}, u32[]{:S(2)}) %collective-permute-start) | collective-permute-done | bytes 4194336 | tf_op jit(solution)/shard_map/ppermute | solution.py:16
  289.4 3.1 collective-permute-done.1
  292.5 11.4 %pad_maximum_fusion.1 = bf16[3072,2048]{1,0:T(8,128)(2,1)} fusion(bf16[1024,2048]{1,0:T(8,128)(2,1)} %collective-permute-done.1, bf16[1024,2048]{1,0:T(8,128)(2,1)} %slice.24, bf16[1024,2048]{1,0:T(8,128)(2,1)} %collective-permute-done), kind=kLoop, calls=%fused_computation.35 | loop fusion | flops 37748736 | bytes 25165824 | tf_op jit(solution)/shard_map/concatenate | solution.py:64
  303.9 287.3 %while.12 = (s32[]{:T(128)}, bf16[4,256,1024]{2,1,0:T(8,128)(2,1)}, s32[4]{0:T(128)S(1)}, bf16[24,128,2048]{2,1,0:T(8,128)(2,1)}, s32[4,2,10]{2,1,0:T(2,128)}, /...) while((s32[]{:T(128)}, bf16[4,256,1024]{2,1,0:T(8,128)(2,1)}, ...), condition=%wide.region_3.4_spmd, body=%wide.region_0.3_spmd.sunk | while | flops 1514416896 | bytes 190909680 | solution.py:77
  305.0 1.3 dynamic-slice_bitcast_fusion.4
  306.3 0.7 compare_select_fusion.2
  307.1 10.0 %gather_fusion = bf16[20,128,2048]{2,1,0:T(8,128)(2,1)} fusion(bf16[24,128,2048]{2,1,0:T(8,128)(2,1)} %get-tuple-element.200, s32[1024]{0:T(1024)S(1)} %pad_clamp_fusion.2), kind=kCustom, calls=%fused_computation.clone.1 | custom fusion | bytes 20971600 | tf_op jit(solution)/shard_map/while/body/eval_jaxpr/gather | solution.py:74
  317.1 10.1 %pad_maximum_fusion.3 = bf16[2,11,128,2048]{3,2,1,0:T(8,128)(2,1)} fusion(bf16[2,10,128,2048]{3,2,1,0:T(8,128)(2,1)} %bitcast.74, bf16[2,1,128,2048]{3,2,1,0:T(8,128)(2,1)S(1)} %dynamic-slice_bitcast_fusion.4), kind=kLoop, calls=%fused_computation.1.clone.1 | loop fusion | flops 5767168 | bytes 23068672 | tf_op jit(solution)/shard_map/while/body/eval_jaxpr/concatenate | solution.py:23
  327.2 9.9 %fusion.40 = (bf16[2,1408,1024]{2,1,0:T(8,128)(2,1)}, bf16[2,1408,1024]{2,1,0:T(8,128)(2,1)}) fusion(bf16[2,1408,2048]{2,1,0:T(8,128)(2,1)} %bitcast.72), kind=kLoop, calls=%fused_computation.38.clone.1 | loop fusion | bytes 23068672 | tf_op jit(solution)/shard_map/while/body/eval_jaxpr/slice | solution.py:25
  337.1 8.3 %copy.26 = bf16[2,1408,1024]{1,2,0:T(8,128)(2,1)} copy(bf16[2,1408,1024]{2,1,0:T(8,128)(2,1)} %get-tuple-element.170) | data formatting | bytes 11534336 | tf_op jit(solution)/shard_map/while/body/eval_jaxpr/slice | solution.py:25
  345.5 1.1 dynamic-slice_bitcast_fusion.5
  346.6 3.9 fusion.42
  350.5 4.2 copy-done.2
  354.7 2.4 fusion.43
  357.1 8.4 %copy.25 = bf16[2,1408,1024]{1,2,0:T(8,128)(2,1)} copy(bf16[2,1408,1024]{2,1,0:T(8,128)(2,1)} %get-tuple-element.169) | data formatting | bytes 11534336 | tf_op jit(solution)/shard_map/while/body/eval_jaxpr/slice | solution.py:26
  365.5 8.8 %divide_convert_fusion.2 = bf16[2,128,8,128]{1,3,2,0:T(8,128)(2,1)S(1)} fusion(bf16[2,1408,8,128]{1,3,2,0:T(8,128)(2,1)} %bitcast.76, f32[2,8,128,1408]{3,2,1,0:T(8,128)} %copy-done.2, f32[2,8,128]{2,1,0:T(8,128)S(1)} %get-tuple-element.172, pred[2,1408]{1,0:T(4,128)(4,1)S(1)} %broadcast_compare_fusion.2, f32[2,128,8]{1,2,0:T(8,128)S(1)} %bitcast.79), kind=kOutput, calls=%fused_computation.13.clone.1 | convolution fusion | flops 750256128 | bytes 17844992 | tf_op jit(solution)/shard_map/while/body/eval_jaxpr/bhqk,bkhd->bqhd/dot_general | solution.py:39
  374.9 0.8 constant_dynamic-update-slice_fusion.2
  376.8 1.3 dynamic-slice_bitcast_fusion.4
  378.2 0.7 compare_select_fusion.2
  378.9 10.0 %gather_fusion = bf16[20,128,2048]{2,1,0:T(8,128)(2,1)} fusion(bf16[24,128,2048]{2,1,0:T(8,128)(2,1)} %get-tuple-element.200, s32[1024]{0:T(1024)S(1)} %pad_clamp_fusion.2), kind=kCustom, calls=%fused_computation.clone.1 | custom fusion | bytes 20971600 | tf_op jit(solution)/shard_map/while/body/eval_jaxpr/gather | solution.py:74
  388.9 10.1 %pad_maximum_fusion.3 = bf16[2,11,128,2048]{3,2,1,0:T(8,128)(2,1)} fusion(bf16[2,10,128,2048]{3,2,1,0:T(8,128)(2,1)} %bitcast.74, bf16[2,1,128,2048]{3,2,1,0:T(8,128)(2,1)S(1)} %dynamic-slice_bitcast_fusion.4), kind=kLoop, calls=%fused_computation.1.clone.1 | loop fusion | flops 5767168 | bytes 23068672 | tf_op jit(solution)/shard_map/while/body/eval_jaxpr/concatenate | solution.py:23
  399.0 9.9 %fusion.40 = (bf16[2,1408,1024]{2,1,0:T(8,128)(2,1)}, bf16[2,1408,1024]{2,1,0:T(8,128)(2,1)}) fusion(bf16[2,1408,2048]{2,1,0:T(8,128)(2,1)} %bitcast.72), kind=kLoop, calls=%fused_computation.38.clone.1 | loop fusion | bytes 23068672 | tf_op jit(solution)/shard_map/while/body/eval_jaxpr/slice | solution.py:25
  408.9 8.3 %copy.26 = bf16[2,1408,1024]{1,2,0:T(8,128)(2,1)} copy(bf16[2,1408,1024]{2,1,0:T(8,128)(2,1)} %get-tuple-element.170) | data formatting | bytes 11534336 | tf_op jit(solution)/shard_map/while/body/eval_jaxpr/slice | solution.py:25
  417.2 1.1 dynamic-slice_bitcast_fusion.5
  418.4 3.9 fusion.42
  422.3 4.2 copy-done.2
  426.5 2.4 fusion.43
  428.9 8.4 %copy.25 = bf16[2,1408,1024]{1,2,0:T(8,128)(2,1)} copy(bf16[2,1408,1024]{2,1,0:T(8,128)(2,1)} %get-tuple-element.169) | data formatting | bytes 11534336 | tf_op jit(solution)/shard_map/while/body/eval_jaxpr/slice | solution.py:26
  437.3 8.8 %divide_convert_fusion.2 = bf16[2,128,8,128]{1,3,2,0:T(8,128)(2,1)S(1)} fusion(bf16[2,1408,8,128]{1,3,2,0:T(8,128)(2,1)} %bitcast.76, f32[2,8,128,1408]{3,2,1,0:T(8,128)} %copy-done.2, f32[2,8,128]{2,1,0:T(8,128)S(1)} %get-tuple-element.172, pred[2,1408]{1,0:T(4,128)(4,1)S(1)} %broadcast_compare_fusion.2, f32[2,128,8]{1,2,0:T(8,128)S(1)} %bitcast.79), kind=kOutput, calls=%fused_computation.13.clone.1 | convolution fusion | flops 750256128 | bytes 17844992 | tf_op jit(solution)/shard_map/while/body/eval_jaxpr/bhqk,bkhd->bqhd/dot_general | solution.py:39
  446.7 0.9 constant_dynamic-update-slice_fusion.2
  448.6 1.3 dynamic-slice_bitcast_fusion.4
  450.0 0.7 compare_select_fusion.2
  450.8 10.0 %gather_fusion = bf16[20,128,2048]{2,1,0:T(8,128)(2,1)} fusion(bf16[24,128,2048]{2,1,0:T(8,128)(2,1)} %get-tuple-element.200, s32[1024]{0:T(1024)S(1)} %pad_clamp_fusion.2), kind=kCustom, calls=%fused_computation.clone.1 | custom fusion | bytes 20971600 | tf_op jit(solution)/shard_map/while/body/eval_jaxpr/gather | solution.py:74
  460.8 10.1 %pad_maximum_fusion.3 = bf16[2,11,128,2048]{3,2,1,0:T(8,128)(2,1)} fusion(bf16[2,10,128,2048]{3,2,1,0:T(8,128)(2,1)} %bitcast.74, bf16[2,1,128,2048]{3,2,1,0:T(8,128)(2,1)S(1)} %dynamic-slice_bitcast_fusion.4), kind=kLoop, calls=%fused_computation.1.clone.1 | loop fusion | flops 5767168 | bytes 23068672 | tf_op jit(solution)/shard_map/while/body/eval_jaxpr/concatenate | solution.py:23
  470.8 9.9 %fusion.40 = (bf16[2,1408,1024]{2,1,0:T(8,128)(2,1)}, bf16[2,1408,1024]{2,1,0:T(8,128)(2,1)}) fusion(bf16[2,1408,2048]{2,1,0:T(8,128)(2,1)} %bitcast.72), kind=kLoop, calls=%fused_computation.38.clone.1 | loop fusion | bytes 23068672 | tf_op jit(solution)/shard_map/while/body/eval_jaxpr/slice | solution.py:25
  480.7 8.3 %copy.26 = bf16[2,1408,1024]{1,2,0:T(8,128)(2,1)} copy(bf16[2,1408,1024]{2,1,0:T(8,128)(2,1)} %get-tuple-element.170) | data formatting | bytes 11534336 | tf_op jit(solution)/shard_map/while/body/eval_jaxpr/slice | solution.py:25
  489.1 1.1 dynamic-slice_bitcast_fusion.5
  490.3 3.9 fusion.42
  494.2 4.2 copy-done.2
  498.3 2.4 fusion.43
  500.8 8.4 %copy.25 = bf16[2,1408,1024]{1,2,0:T(8,128)(2,1)} copy(bf16[2,1408,1024]{2,1,0:T(8,128)(2,1)} %get-tuple-element.169) | data formatting | bytes 11534336 | tf_op jit(solution)/shard_map/while/body/eval_jaxpr/slice | solution.py:26
  509.1 8.8 %divide_convert_fusion.2 = bf16[2,128,8,128]{1,3,2,0:T(8,128)(2,1)S(1)} fusion(bf16[2,1408,8,128]{1,3,2,0:T(8,128)(2,1)} %bitcast.76, f32[2,8,128,1408]{3,2,1,0:T(8,128)} %copy-done.2, f32[2,8,128]{2,1,0:T(8,128)S(1)} %get-tuple-element.172, pred[2,1408]{1,0:T(4,128)(4,1)S(1)} %broadcast_compare_fusion.2, f32[2,128,8]{1,2,0:T(8,128)S(1)} %bitcast.79), kind=kOutput, calls=%fused_computation.13.clone.1 | convolution fusion | flops 750256128 | bytes 17844992 | tf_op jit(solution)/shard_map/while/body/eval_jaxpr/bhqk,bkhd->bqhd/dot_general | solution.py:39
  518.5 0.8 constant_dynamic-update-slice_fusion.2
  520.5 1.3 dynamic-slice_bitcast_fusion.4
  521.8 0.7 compare_select_fusion.2
  522.6 10.0 %gather_fusion = bf16[20,128,2048]{2,1,0:T(8,128)(2,1)} fusion(bf16[24,128,2048]{2,1,0:T(8,128)(2,1)} %get-tuple-element.200, s32[1024]{0:T(1024)S(1)} %pad_clamp_fusion.2), kind=kCustom, calls=%fused_computation.clone.1 | custom fusion | bytes 20971600 | tf_op jit(solution)/shard_map/while/body/eval_jaxpr/gather | solution.py:74
  532.6 10.1 %pad_maximum_fusion.3 = bf16[2,11,128,2048]{3,2,1,0:T(8,128)(2,1)} fusion(bf16[2,10,128,2048]{3,2,1,0:T(8,128)(2,1)} %bitcast.74, bf16[2,1,128,2048]{3,2,1,0:T(8,128)(2,1)S(1)} %dynamic-slice_bitcast_fusion.4), kind=kLoop, calls=%fused_computation.1.clone.1 | loop fusion | flops 5767168 | bytes 23068672 | tf_op jit(solution)/shard_map/while/body/eval_jaxpr/concatenate | solution.py:23
  542.6 9.9 %fusion.40 = (bf16[2,1408,1024]{2,1,0:T(8,128)(2,1)}, bf16[2,1408,1024]{2,1,0:T(8,128)(2,1)}) fusion(bf16[2,1408,2048]{2,1,0:T(8,128)(2,1)} %bitcast.72), kind=kLoop, calls=%fused_computation.38.clone.1 | loop fusion | bytes 23068672 | tf_op jit(solution)/shard_map/while/body/eval_jaxpr/slice | solution.py:25
  552.6 8.3 %copy.26 = bf16[2,1408,1024]{1,2,0:T(8,128)(2,1)} copy(bf16[2,1408,1024]{2,1,0:T(8,128)(2,1)} %get-tuple-element.170) | data formatting | bytes 11534336 | tf_op jit(solution)/shard_map/while/body/eval_jaxpr/slice | solution.py:25
  560.9 1.1 dynamic-slice_bitcast_fusion.5
  562.1 3.9 fusion.42
  566.0 4.2 copy-done.2
  570.2 2.4 fusion.43
  572.6 8.4 %copy.25 = bf16[2,1408,1024]{1,2,0:T(8,128)(2,1)} copy(bf16[2,1408,1024]{2,1,0:T(8,128)(2,1)} %get-tuple-element.169) | data formatting | bytes 11534336 | tf_op jit(solution)/shard_map/while/body/eval_jaxpr/slice | solution.py:26
  580.9 8.8 %divide_convert_fusion.2 = bf16[2,128,8,128]{1,3,2,0:T(8,128)(2,1)S(1)} fusion(bf16[2,1408,8,128]{1,3,2,0:T(8,128)(2,1)} %bitcast.76, f32[2,8,128,1408]{3,2,1,0:T(8,128)} %copy-done.2, f32[2,8,128]{2,1,0:T(8,128)S(1)} %get-tuple-element.172, pred[2,1408]{1,0:T(4,128)(4,1)S(1)} %broadcast_compare_fusion.2, f32[2,128,8]{1,2,0:T(8,128)S(1)} %bitcast.79), kind=kOutput, calls=%fused_computation.13.clone.1 | convolution fusion | flops 750256128 | bytes 17844992 | tf_op jit(solution)/shard_map/while/body/eval_jaxpr/bhqk,bkhd->bqhd/dot_general | solution.py:39
  590.3 0.8 constant_dynamic-update-slice_fusion.2
  591.1 6.0 convolution_convert_fusion.1
  (55 shorter events, 5.6 us)
Async XLA Ops:
  6.5 135.1 %copy-start = (bf16[1024,1024]{1,0:T(8,128)(2,1)S(1)}, bf16[1024,1024]{1,0:T(8,128)(2,1)}, u32[]{:S(2)}) copy-start(bf16[1024,1024]{1,0:T(8,128)(2,1)} %param.7) | copy-start | bytes 6291460
  6.5 135.1 %all-gather.3.cloned.1.call-start = ((), (), s32[]{:S(2)}) async-start(), calls=%async_computation | async-start | bytes 7077888 | tf_op jit(solution)/shard_map/all_gather | solution.py:54
  7.3 583.9 %all-gather.5.cloned.1.call-start = ((), (), s32[]{:S(2)}) async-start(), calls=%async_computation.1 | async-start | bytes 2359296 | tf_op jit(solution)/shard_map/all_gather | solution.py:89
  151.3 2.7 copy-start.3
  153.9 5.5 copy-start.4
  156.2 133.3 %collective-permute-start = (bf16[1024,2048]{1,0:T(8,128)(2,1)}, bf16[1024,2048]{1,0:T(8,128)(2,1)}, u32[]{:S(2)}, u32[]{:S(2)}) collective-permute-start(bf16[1024,2048]{1,0:T(8,128)(2,1)} %slice.24), channel_id=1, source_target_pairs={{0,8},{8,16},{16,24},{24,32},{32,40},{40,48},{48,56},{56,64},{64,7... | collective-permute-start | bytes 12582920 | tf_op jit(solution)/shard_map/ppermute | solution.py:16
  159.4 133.1 %collective-permute-start.1 = (bf16[1024,2048]{1,0:T(8,128)(2,1)}, bf16[1024,2048]{1,0:T(8,128)(2,1)}, u32[]{:S(2)}, u32[]{:S(2)}) collective-permute-start(bf16[1024,2048]{1,0:T(8,128)(2,1)} %slice.24), channel_id=1, source_target_pairs={{0,120},{8,0},{16,8},{24,16},{32,24},{40,32},{48,40},{56,48},{64,5... | collective-permute-start | bytes 12582920 | tf_op jit(solution)/shard_map/ppermute | solution.py:16
  350.5 4.2 copy-start.2
  422.3 4.2 copy-start.2
  494.2 4.2 copy-start.2
  566.0 4.2 copy-start.2
  591.1 6.0 copy-start.1
Sparse Core Ops, SparseCore 0:
  9.0 132.5 all-gather.2
  159.5 109.6 all-gather.4
where the time goes:
time: 607 us; the launch traced here: 604 us
  waiting for transfers between devices  265 us (44%)
  local copies, waits for them, and re-layouts  189 us (31%)
  matrix products  66.5 us (11%)
  other arithmetic  64.4 us (11%)
  between operations  13.4 us (2%)
    all_gather x1, waiting for transfers between devices, shards(): lax.all_gather(w_qkv, 'fsdp', axis=0, tiled=True)  134 us
    ppermute x2, waiting for transfers between devices, from_behind(): return lax.ppermute(value, axis, pairs)  130 us
    slice x8, local copies, waits for them, and re-layouts, attend(): keyvals[..., :feature_width].reshape(block_count, -1, HEADS, head_width)  72.8 us
    concatenate x4, other arithmetic, attend(): keyvals = jnp.concatenate([own_blocks[:, None], picked], axis=1)  40.2 us
    gather x4, local copies, waits for them, and re-layouts, one_group(): picked = pool[layout_part]  40 us
    dot_general x4, matrix products, attend(): jnp.einsum('bhqk,bkhd->bqhd', rounded, value_heads, preferred_element_typ...  35.3 us
    slice x4, local copies, waits for them, and re-layouts, attend(): keyvals[..., feature_width:].reshape(block_count, -1, HEADS, head_width)  33.5 us
    while x16, local copies, waits for them, and re-layouts  21.4 us
  transfers between devices with their start and end apart: 4, of which 3 were waited for; matrix products, arithmetic and copies ran while one was open for 47% of the time, Pallas kernels for 0%

commit v1 on v0

v1 whole, which is shorter than its diff:
```python
import functools

import jax
import jax.numpy as jnp
from jax import lax
from jax.experimental import pallas as pl
from jax.experimental.pallas import tpu as pltpu
from jax.sharding import PartitionSpec as P

HEADS = 8
BLOCK = 128
HEAD = 128
MESH = pl.DeviceIdType.MESH
LOG2E = 1.4426950408889634
NEG = float("-inf")
F32 = jnp.float32
BF16 = jnp.bfloat16


def from_behind(value, axis, steps):
    count = lax.axis_size(axis)
    pairs = [(source, (source + steps) % count) for source in range(count)]
    return lax.ppermute(value, axis, pairs)


def gather_kernel(wq, wo, gq, go, send, recv, send2, recv2, own):
    s = lax.axis_index("seq")
    f = lax.axis_index("fsdp")
    core = lax.rem(s, 2)
    mate = (s + 1 - 2 * core, f)
    y = lax.rem(f, 2)
    z = f // 2
    up, down, far = lax.rem(z + 1, 4), lax.rem(z + 3, 4), lax.rem(z + 2, 4)
    dev_y, dev_up, dev_down = (s, 2 * z + 1 - y), (s, 2 * up + y), (s, 2 * down + y)
    barrier = pltpu.get_barrier_semaphore()
    for peer in (dev_y, dev_up, dev_down, mate):
        pl.semaphore_signal(barrier, inc=1, device_id=peer, device_id_type=MESH)
    pl.semaphore_wait(barrier, 4)
    rows = gq.shape[0] // 8
    half = rows // 2

    started = []
    for a, (w, g) in enumerate(((wq, gq), (wo, go))):
        mine = pltpu.make_async_copy(w, g.at[pl.ds(pl.multiple_of(f * rows, rows), rows)], own.at[a])
        mine.start()
        started.append(mine)

    def part(owner, offset, count):
        return pl.ds(pl.multiple_of(owner * rows + core * half + offset, 32), count)

    for a, (w, g) in enumerate(((wq, gq), (wo, go))):
        def send_to(k, owner, offset, count, peer, local):
            place = part(owner, offset, count)
            source = w.at[pl.ds(pl.multiple_of(core * half, 32), half)] if local else g.at[place]
            copy = pltpu.make_async_remote_copy(
                source, g.at[place], send.at[a, k], recv.at[a, k], device_id=peer, device_id_type=MESH)
            copy.start()
            return copy

        def hand(k, owner):
            place = part(owner, 0, half)
            copy = pltpu.make_async_remote_copy(
                g.at[place], g.at[place], send2.at[a, k], recv2.at[a, k], device_id=mate, device_id_type=MESH)
            copy.start()
            return copy

        own_y = 2 * z + 1 - y
        c_y = send_to(0, f, 0, half, dev_y, True)
        c_u0 = send_to(1, f, 0, half, dev_up, True)
        c_d0 = send_to(2, f, 0, half, dev_down, True)
        c_y.wait_recv()
        c_u1 = send_to(3, own_y, 0, half, dev_up, False)
        c_d1 = send_to(4, own_y, 0, half, dev_down, False)
        hands = [hand(0, own_y)]
        c_u0.wait_recv()
        c_u2 = send_to(5, 2 * down + y, 0, half // 2, dev_up, False)
        hands.append(hand(1, 2 * down + y))
        c_d0.wait_recv()
        c_d2 = send_to(6, 2 * up + y, half // 2, half // 2, dev_down, False)
        hands.append(hand(2, 2 * up + y))
        c_u1.wait_recv()
        c_u3 = send_to(7, 2 * down + 1 - y, 0, half // 2, dev_up, False)
        hands.append(hand(3, 2 * down + 1 - y))
        c_d1.wait_recv()
        c_d3 = send_to(8, 2 * up + 1 - y, half // 2, half // 2, dev_down, False)
        hands.append(hand(4, 2 * up + 1 - y))
        c_u2.wait_recv()
        c_d2.wait_recv()
        hands.append(hand(5, 2 * far + y))
        c_u3.wait_recv()
        c_d3.wait_recv()
        hands.append(hand(6, 2 * far + 1 - y))
        for copy in (c_y, c_u0, c_d0, c_u1, c_d1, c_u2, c_d2, c_u3, c_d3):
            copy.wait_send()
        for copy in hands:
            copy.wait()
    for copy in started:
        copy.wait()


def gather_weights(w_qkv, w_out):
    hbm = pl.BlockSpec(memory_space=pl.ANY)
    dma = pltpu.SemaphoreType.DMA
    return pl.pallas_call(
        gather_kernel,
        out_shape=[
            jax.ShapeDtypeStruct((8 * w_qkv.shape[0], w_qkv.shape[1]), BF16),
            jax.ShapeDtypeStruct((8 * w_out.shape[0], w_out.shape[1]), BF16),
        ],
        in_specs=[hbm, hbm],
        out_specs=[hbm, hbm],
        scratch_shapes=[dma((2, 9)), dma((2, 9)), dma((2, 7)), dma((2, 7)), dma((2,))],
        compiler_params=pltpu.CompilerParams(collective_id=0, has_side_effects=True),
        name="gather_weights",
    )(w_qkv, w_out)


def nt_dot(a, b):
    return lax.dot_general(a, b, (((1,), (1,)), ((), ())), preferred_element_type=F32)


def attention_kernel(layout, counts, q_ref, k_ref, v_ref, wo_ref, o_ref, s_sc, m_sc, l_sc, a_sc, att):
    scale = HEAD ** -0.5 * LOG2E
    lane = lax.broadcasted_iota(jnp.int32, (1, 2 * BLOCK), 1)
    slots = layout.shape[1]

    def block(b, _):
        used = counts[b] + 1
        pairs = (used + 1) // 2
        rows = pl.ds(pl.multiple_of(b * BLOCK, BLOCK), BLOCK)
        for h in range(HEADS):
            m_sc[h] = jnp.full((BLOCK, BLOCK), NEG, F32)
            l_sc[h] = jnp.zeros((BLOCK, BLOCK), F32)
            a_sc[h] = jnp.zeros((BLOCK, HEAD), F32)

        def entries(i):
            first = jnp.where(i == 0, 8 + b, layout[b, jnp.maximum(2 * i - 1, 0)])
            return first, layout[b, jnp.minimum(2 * i, slots - 1)]

        def score(i, _):
            e0, e1 = entries(i)
            bias = jnp.where((lane >= BLOCK) & (2 * i + 1 >= used), NEG, 0.0)
            for h in range(HEADS):
                cols = slice(h * HEAD, (h + 1) * HEAD)
                keys = jnp.concatenate([k_ref[e0, :, cols], k_ref[e1, :, cols]], axis=0)
                s = nt_dot(q_ref[rows, cols], keys) + bias
                s_sc[i, h] = s
                m_sc[h] = jnp.maximum(m_sc[h], jnp.maximum(s[:, :BLOCK], s[:, BLOCK:]))
            return 0

        lax.fori_loop(0, pairs, score, 0)
        for h in range(HEADS):
            m_sc[h] = jnp.broadcast_to(jnp.max(m_sc[h], axis=1, keepdims=True) * scale, (BLOCK, BLOCK))

        def weigh(i, _):
            e0, e1 = entries(i)
            for h in range(HEADS):
                cols = slice(h * HEAD, (h + 1) * HEAD)
                values = jnp.concatenate([v_ref[e0, :, cols], v_ref[e1, :, cols]], axis=0)
                s = s_sc[i, h]
                m = m_sc[h]
                p0 = jnp.exp2(s[:, :BLOCK] * scale - m)
                p1 = jnp.exp2(s[:, BLOCK:] * scale - m)
                l_sc[h] += p0 + p1
                p = jnp.concatenate([p0.astype(BF16), p1.astype(BF16)], axis=1)
                a_sc[h] += jnp.dot(p, values, preferred_element_type=F32)
            return 0

        lax.fori_loop(0, pairs, weigh, 0)
        for h in range(HEADS):
            total = jnp.sum(l_sc[h], axis=1, keepdims=True)
            att[rows, h * HEAD:(h + 1) * HEAD] = (a_sc[h] / total).astype(BF16)
        return 0

    lax.fori_loop(0, q_ref.shape[0] // BLOCK, block, 0)
    for c in range(0, o_ref.shape[1], 256):
        o_ref[:, c:c + 256] = jnp.dot(att[...], wo_ref[:, c:c + 256], preferred_element_type=F32).astype(BF16)


def attention(q, k, v, w_out, layout, counts):
    vmem = pl.BlockSpec(memory_space=pltpu.VMEM)
    smem = pl.BlockSpec(memory_space=pltpu.SMEM)
    pairs = layout.shape[1] // 2 + 1
    return pl.pallas_call(
        attention_kernel,
        out_shape=jax.ShapeDtypeStruct(q.shape, BF16),
        in_specs=[smem, smem, vmem, vmem, vmem, vmem],
        out_specs=vmem,
        scratch_shapes=[
            pltpu.VMEM((pairs, HEADS, BLOCK, 2 * BLOCK), F32),
            pltpu.VMEM((HEADS, BLOCK, BLOCK), F32),
            pltpu.VMEM((HEADS, BLOCK, BLOCK), F32),
            pltpu.VMEM((HEADS, BLOCK, HEAD), F32),
            pltpu.VMEM(q.shape, BF16),
        ],
        compiler_params=pltpu.CompilerParams(vmem_limit_bytes=56 << 20),
        name="attention",
    )(layout, counts, q, k, v, w_out)


def shards(normed, w_qkv, w_out, layout, counts):
    width = normed.shape[1]
    lower = from_behind(normed, "seq", 1)
    upper = from_behind(normed, "seq", -1)
    full_qkv, full_out = gather_weights(w_qkv, w_out)
    pool = jnp.concatenate([lower, normed, upper], axis=0)
    queries = jnp.dot(normed, full_qkv[:, :width], preferred_element_type=F32).astype(BF16)
    keys = jnp.dot(pool, full_qkv[:, width:2 * width], preferred_element_type=F32).astype(BF16)
    values = jnp.dot(pool, full_qkv[:, 2 * width:], preferred_element_type=F32).astype(BF16)
    shape = (-1, BLOCK, width)
    return attention(queries, keys.reshape(shape), values.reshape(shape), full_out, layout, counts)


def solution(mesh):
    return jax.shard_map(
        shards,
        mesh=mesh,
        in_specs=(
            P(("seq", "fsdp"), None),
            P("fsdp", None),
            P("fsdp", None),
            P(("seq", "fsdp"), None),
            P(("seq", "fsdp")),
        ),
        out_specs=P(("seq", "fsdp"), None),
        check_vma=False,
    )
```

time: 607 us -> 158 us (0.26)
  the two profiles are of different devices: /device:TPU:1 before, /device:TPU:61 now
where the time goes in v1:
time: 158 us
  Pallas kernels  128 us (81%)
  matrix products  24.2 us (15%)
  local copies, waits for them, and re-layouts  3.7 us (2%)
  starting transfers between devices  2.15 us (1%)
    pallas_call x1, Pallas kernels, gather_weights(): pl.pallas_call(gather_kernel, out_shape=[jax.ShapeDtypeStruct((8 * w_qkv....  89.7 us
    pallas_call x1, Pallas kernels, attention(): pl.pallas_call(attention_kernel, out_shape=jax.ShapeDtypeStruct(q.shape,...  38.5 us
    dot_general x1, matrix products, shards(): jnp.dot(pool, full_qkv[:, 2 * width:], preferred_element_type=F32)  9.09 us
    dot_general x1, matrix products, shards(): jnp.dot(pool, full_qkv[:, width:2 * width], preferred_element_type=F32)  9.07 us
    dot_general x1, matrix products, shards(): jnp.dot(normed, full_qkv[:, :width], preferred_element_type=F32)  6.01 us
    unnamed x8, local copies, waits for them, and re-layouts  3.53 us
  transfers between devices with their start and end apart: 2, of which 0 were waited for; matrix products, arithmetic and copies ran while one was open for 5% of the time, Pallas kernels for 57%

profile of v1, /device:TPU:61, one launch (start us, length us, event | category | flops | bytes accessed | tf_op | source)
XLA Modules:
  0.0 158.3 jit_solution(17455210845087455142)
XLA Ops:
  0.0 2.1 %collective-permute-start = (bf16[1024,1024]{1,0:T(8,128)(2,1)}, bf16[1024,1024]{1,0:T(8,128)(2,1)}, u32[]{:S(2)}, u32[]{:S(2)}) collective-permute-start(bf16[1024,1024]{1,0:T(8,128)(2,1)} %param.5), channel_id=1, source_target_pairs={{0,8},{8,16},{16,24},{24,32},{32,40},{40,48},{48,56},{56,64},{64,7... | collective-permute-start | bytes 6291464 | tf_op jit(solution)/shard_map/ppermute | solution.py:23
  2.1 0.0 collective-permute-start.1
  2.2 89.7 %gather_weights.1 = (bf16[1024,3072]{1,0:T(8,128)(2,1)}, bf16[1024,1024]{1,0:T(8,128)(2,1)}) custom-call(bf16[128,3072]{1,0:T(8,128)(2,1)} %wq.1, bf16[128,1024]{1,0:T(8,128)(2,1)} %wo.1), custom_call_target="tpu_custom_call" | custom-call | tf_op jit(solution)/shard_map/gather_weights/pallas_call | solution.py:104
  91.9 0.0 copy-start
  91.9 6.0 %convert_bitcast_fusion.q_ref = bf16[1024,1024]{1,0:T(8,128)(2,1)} fusion(bf16[1024,1024]{1,0:T(8,128)(2,1)} %param.5, bf16[1024,3072]{1,0:T(8,128)(2,1)} %get-tuple-element.7), kind=kOutput, calls=%fused_computation.4 | convolution fusion | flops 2148532224 | bytes 6291456 | tf_op jit(solution)/shard_map/dot_general | solution.py:207
  97.9 0.0 slice-start
  97.9 0.0 collective-permute-done
  97.9 1.9 %constant_dynamic-update-slice_fusion.2 = bf16[3072,1024]{1,0:T(8,128)(2,1)S(1)} fusion(bf16[1024,1024]{1,0:T(8,128)(2,1)} %collective-permute-done), kind=kLoop, calls=%fused_computation.9 | loop fusion | bytes 4194304
  99.9 0.0 copy-done
  99.9 0.0 slice-start.1
  99.9 0.2 constant_dynamic-update-slice_fusion.1
  100.1 0.0 collective-permute-done.1
  100.1 0.2 constant_dynamic-update-slice_fusion
  100.3 0.5 slice-done
  100.8 0.9 slice-done.1
  101.7 9.1 %convolution_convert_fusion.1 = bf16[3072,1024]{1,0:T(8,128)(2,1)} fusion(bf16[3072,1024]{1,0:T(8,128)(2,1)S(1)} %constant_dynamic-update-slice_fusion, bf16[1024,3072]{1,0:T(8,128)(2,1)S(1)} %bitcast.10), kind=kOutput, calls=%fused_computation.1 | convolution fusion | flops 6445596672 | bytes 14680064 | tf_op jit(solution)/shard_map/dot_general | solution.py:208
  110.8 9.1 %convolution_convert_fusion = bf16[3072,1024]{1,0:T(8,128)(2,1)} fusion(bf16[3072,1024]{1,0:T(8,128)(2,1)S(1)} %constant_dynamic-update-slice_fusion, bf16[1024,3072]{1,0:T(8,128)(2,1)S(1)} %bitcast.10), kind=kOutput, calls=%fused_computation | convolution fusion | flops 6445596672 | bytes 14680064 | tf_op jit(solution)/shard_map/dot_general | solution.py:209
  119.8 38.5 %attention.1 = bf16[1024,1024]{1,0:T(8,128)(2,1)} custom-call(s32[8,10]{1,0:T(8,128)} %layout.1, s32[8]{0:T(128)} %counts.1, bf16[1024,1024]{1,0:T(8,128)(2,1)} %convert_bitcast_fusion.q_ref, bf16[24,128,1024]{2,1,0:T(8,128)(2,1)} %bitcast.7, bf16[24,128,1024]{2,1,0:T(8,128)(2,1)} %bitcast.8, bf16[1024,1024]{1,0:T(8,128)(2,1)} %get-tuple-element.8.wo_ref), custom_call_target="tpu_custom_call" | custom-call | tf_op jit(solution)/shard_map/attention/pallas_call | solution.py:184
  (1 shorter events, 0.0 us)
Async XLA Ops:
  0.0 97.9 %collective-permute-start = (bf16[1024,1024]{1,0:T(8,128)(2,1)}, bf16[1024,1024]{1,0:T(8,128)(2,1)}, u32[]{:S(2)}, u32[]{:S(2)}) collective-permute-start(bf16[1024,1024]{1,0:T(8,128)(2,1)} %param.5), channel_id=1, source_target_pairs={{0,8},{8,16},{16,24},{24,32},{32,40},{40,48},{48,56},{56,64},{64,7... | collective-permute-start | bytes 6291464 | tf_op jit(solution)/shard_map/ppermute | solution.py:23
  2.1 97.9 %collective-permute-start.1 = (bf16[1024,1024]{1,0:T(8,128)(2,1)}, bf16[1024,1024]{1,0:T(8,128)(2,1)S(1)}, u32[]{:S(2)}, u32[]{:S(2)}) collective-permute-start(bf16[1024,1024]{1,0:T(8,128)(2,1)} %param.5), channel_id=1, source_target_pairs={{0,120},{8,0},{16,8},{24,16},{32,24},{40,32},{48,40},{56,48},{64,5... | collective-permute-start | bytes 6291464 | tf_op jit(solution)/shard_map/ppermute | solution.py:23
  91.9 8.0 %copy-start = (bf16[1024,1024]{1,0:T(8,128)(2,1)S(1)}, bf16[1024,1024]{1,0:T(8,128)(2,1)}, u32[]{:S(2)}) copy-start(bf16[1024,1024]{1,0:T(8,128)(2,1)} %param.5) | copy-start | bytes 6291460
  97.9 2.8 %slice-start = ((s8[6291456]{0:T(1024)(128)(4,1)}), s8[4194304]{0:T(1024)(128)(4,1)S(1)}, s32[]{:S(2)}) async-start(s8[6291456]{0:T(1024)(128)(4,1)} %bitcast.9), calls=%async_computation | async-start | bytes 8388608
  99.9 1.8 %slice-start.1 = ((s8[6291456]{0:T(1024)(128)(4,1)}), s8[2097152]{0:T(1024)(128)(4,1)S(1)}, s32[]{:S(2)}) async-start(s8[6291456]{0:T(1024)(128)(4,1)} %bitcast.9), calls=%async_computation.1 | async-start | bytes 4194304

commit v2 on v1

v2 whole, which is shorter than its diff:
```python
import functools

import jax
import jax.numpy as jnp
from jax import lax
from jax.experimental import pallas as pl
from jax.experimental.pallas import tpu as pltpu
from jax.sharding import PartitionSpec as P

HEADS = 8
BLOCK = 128
HEAD = 128
MESH = pl.DeviceIdType.MESH
LOG2E = 1.4426950408889634
NEG = float("-inf")
F32 = jnp.float32
BF16 = jnp.bfloat16


def project_kernel(x, wq_shard, wo_shard, q_out, k_out, v_out, wo_out, wq, inner, outer, stage_q, stage_kv, send, recv,
                   send2, recv2, own, x_send, x_recv, store):
    s = lax.axis_index("seq")
    f = lax.axis_index("fsdp")
    count = lax.axis_size("seq")
    core = lax.rem(s, 2)
    side = 2 * core - 1
    mate = (s - side, f)
    beyond = (lax.rem(s + side + count, count), f)
    y = lax.rem(f, 2)
    z = f // 2
    fy = 2 * z + 1 - y
    s_flip = s + 2 - 4 * lax.rem(s // 2, 2)
    up, down, far = lax.rem(z + 1, 4), lax.rem(z + 3, 4), lax.rem(z + 2, 4)
    dev_y, dev_y2, dev_up, dev_down = (s, fy), (s_flip, fy), (s, 2 * up + y), (s, 2 * down + y)
    barrier = pltpu.get_barrier_semaphore()
    for peer in (dev_y, dev_y2, dev_up, dev_down, mate, beyond):
        pl.semaphore_signal(barrier, inc=1, device_id=peer, device_id_type=MESH)
    pl.semaphore_wait(barrier, 6)
    rows = wq_shard.shape[0]
    half = rows // 2
    quarter = rows // 4
    arrays = ((wq_shard, wq), (wo_shard, wo_out))
    pending = []

    def start(copy):
        copy.start()
        return copy

    def part(owner, offset, size):
        return pl.ds(pl.multiple_of(owner * rows + core * half + offset, quarter), size)

    def send_to(a, k, owner, offset, size, peer, local):
        shard, full = arrays[a]
        place = part(owner, offset, size)
        source = shard.at[pl.ds(pl.multiple_of(core * half + offset, quarter), size)] if local else full.at[place]
        copy = start(pltpu.make_async_remote_copy(
            source, full.at[place], send.at[a, k], recv.at[a, k], device_id=peer, device_id_type=MESH))
        pending.append(copy)
        return copy

    def hand(a, k, owner):
        full = arrays[a][1]
        place = part(owner, 0, half)
        return start(pltpu.make_async_remote_copy(
            full.at[place], full.at[place], send2.at[a, k], recv2.at[a, k], device_id=mate, device_id_type=MESH))

    def send_y(a):
        return (send_to(a, 0, f, 0, quarter, dev_y, True), send_to(a, 9, f, quarter, quarter, dev_y2, True))

    def send_own(a):
        return (send_to(a, 1, f, 0, half, dev_up, True), send_to(a, 2, f, 0, half, dev_down, True))

    def send_other(a):
        return (send_to(a, 3, fy, 0, half, dev_up, False), send_to(a, 4, fy, 0, half, dev_down, False))

    def onward(a, first, odd):
        lane = 1 - y if odd else y
        k = 7 if odd else 5
        h = 3 if odd else 1
        first[0].wait_recv()
        c_up = send_to(a, k, 2 * down + lane, 0, quarter, dev_up, False)
        h_up = hand(a, h, 2 * down + lane)
        first[1].wait_recv()
        c_down = send_to(a, k + 1, 2 * up + lane, quarter, quarter, dev_down, False)
        return (c_up, c_down), [h_up, hand(a, h + 1, 2 * up + lane)]

    def last(a, second, odd):
        second[0].wait_recv()
        second[1].wait_recv()
        return [hand(a, 6 if odd else 5, 2 * far + (1 - y if odd else y))]

    y_q = send_y(0)
    own_q = send_own(0)
    place = pl.ds(pl.multiple_of(f * rows, rows), rows)
    own_copy_q, own_copy_o = [
        start(pltpu.make_async_copy(shard, full.at[place], own.at[a])) for a, (shard, full) in enumerate(arrays)]
    y_o = send_y(1)
    inner_copy = start(pltpu.make_async_remote_copy(
        x, inner, x_send.at[8], x_recv.at[8], device_id=mate, device_id_type=MESH))
    for copy in y_q:
        copy.wait_recv()
    other_q = send_other(0)
    hands_q = [hand(0, 0, fy)]
    for copy in y_o:
        copy.wait_recv()
    step = x.shape[0] // 8
    outer_copies = []
    for i in range(8):
        place = pl.ds(i * step, step)
        outer_copies.append(start(pltpu.make_async_remote_copy(
            x.at[place], outer.at[place], x_send.at[i], x_recv.at[i], device_id=beyond, device_id_type=MESH)))
    onward_q, more = onward(0, own_q, False)
    hands_q += more
    onward_q2, more = onward(0, other_q, True)
    hands_q += more
    own_o = send_own(1)
    other_o = send_other(1)
    hands_o = [hand(1, 0, fy)]
    hands_q += last(0, onward_q, False)
    hands_q += last(0, onward_q2, True)
    own_copy_q.wait()
    for copy in hands_q:
        copy.wait_recv()

    width = x.shape[1]
    tile = 256
    total = x.shape[0]

    def project(source, target, offset, columns):
        def one(n, _):
            cols = pl.ds(pl.multiple_of(n * tile, tile), tile)
            w_cols = pl.ds(pl.multiple_of(offset + n * tile, tile), tile)
            target[:, cols] = jnp.dot(source[...], wq[:, w_cols], preferred_element_type=F32).astype(BF16)
            return 0

        lax.fori_loop(0, columns // tile, one, 0)

    stores = []

    def keep(source, target, k):
        copy = pltpu.make_async_copy(source, target, store.at[k])
        copy.start()
        stores.append(copy)

    def keep_kv(source, base, size, k):
        place = pl.ds(pl.multiple_of(base, size), size)
        keep(source.at[:, pl.ds(0, width)], k_out.at[place], k)
        keep(source.at[:, pl.ds(width, width)], v_out.at[place], k + 1)

    project(x, stage_q, 0, width)
    keep(stage_q, q_out, 0)
    onward_o, more = onward(1, own_o, False)
    hands_o += more
    project(x, stage_kv.at[pl.ds(0, total)], width, 2 * width)
    keep_kv(stage_kv.at[pl.ds(0, total)], total, total, 1)
    onward_o2, more = onward(1, other_o, True)
    hands_o += more
    inner_copy.wait_recv()
    project(inner, stage_kv.at[pl.ds(total, total)], width, 2 * width)
    keep_kv(stage_kv.at[pl.ds(total, total)], (1 - core) * 2 * total, total, 3)
    hands_o += last(1, onward_o, False)
    hands_o += last(1, onward_o2, True)
    for i in range(4):
        outer_copies[2 * i].wait_recv()
        outer_copies[2 * i + 1].wait_recv()
        piece = pl.ds(2 * i * step, 2 * step)
        staged = stage_kv.at[pl.ds(2 * total + 2 * i * step, 2 * step)]
        project(outer.at[piece], staged, width, 2 * width)
        keep_kv(staged, core * 2 * total + 2 * i * step, 2 * step, 5 + 2 * i)
    own_copy_o.wait()
    for copy in hands_o:
        copy.wait_recv()
    for copy in pending + hands_q + hands_o + outer_copies + [inner_copy]:
        copy.wait_send()
    for copy in stores:
        copy.wait()


def project_all(x, w_qkv, w_out):
    hbm = pl.BlockSpec(memory_space=pl.ANY)
    vmem = pl.BlockSpec(memory_space=pltpu.VMEM)
    dma = pltpu.SemaphoreType.DMA
    rows, width = x.shape
    return pl.pallas_call(
        project_kernel,
        out_shape=[
            jax.ShapeDtypeStruct((rows, width), BF16),
            jax.ShapeDtypeStruct((3 * rows, width), BF16),
            jax.ShapeDtypeStruct((3 * rows, width), BF16),
            jax.ShapeDtypeStruct((8 * w_out.shape[0], width), BF16),
        ],
        in_specs=[vmem, hbm, hbm],
        out_specs=[hbm, hbm, hbm, hbm],
        scratch_shapes=[
            pltpu.VMEM((8 * w_qkv.shape[0], w_qkv.shape[1]), BF16),
            pltpu.VMEM((rows, width), BF16),
            pltpu.VMEM((rows, width), BF16),
            pltpu.VMEM((rows, width), BF16),
            pltpu.VMEM((3 * rows, 2 * width), BF16),
            dma((2, 10)), dma((2, 10)), dma((2, 7)), dma((2, 7)), dma((2,)), dma((9,)), dma((9,)), dma((13,)),
        ],
        compiler_params=pltpu.CompilerParams(
            collective_id=0, has_side_effects=True, vmem_limit_bytes=48 << 20),
        name="gather_and_project",
    )(x, w_qkv, w_out)


def nt_dot(a, b):
    return lax.dot_general(a, b, (((1,), (1,)), ((), ())), preferred_element_type=F32)


def attention_kernel(layout, counts, q_ref, k_ref, v_ref, wo_ref, o_ref, s_sc, m_sc, l_sc, a_sc, att):
    scale = HEAD ** -0.5 * LOG2E
    lane = lax.broadcasted_iota(jnp.int32, (1, 2 * BLOCK), 1)
    slots = layout.shape[1]

    def block(b, _):
        used = counts[b] + 1
        pairs = (used + 1) // 2
        rows = pl.ds(pl.multiple_of(b * BLOCK, BLOCK), BLOCK)
        for h in range(HEADS):
            m_sc[h] = jnp.full((BLOCK, BLOCK), NEG, F32)
            l_sc[h] = jnp.zeros((BLOCK, BLOCK), F32)
            a_sc[h] = jnp.zeros((BLOCK, HEAD), F32)

        def entries(i):
            first = jnp.where(i == 0, 8 + b, layout[b, jnp.maximum(2 * i - 1, 0)])
            return first, layout[b, jnp.minimum(2 * i, slots - 1)]

        def score(i, _):
            e0, e1 = entries(i)
            bias = jnp.where((lane >= BLOCK) & (2 * i + 1 >= used), NEG, 0.0)
            for h in range(HEADS):
                cols = slice(h * HEAD, (h + 1) * HEAD)
                keys = jnp.concatenate([k_ref[e0, :, cols], k_ref[e1, :, cols]], axis=0)
                s = nt_dot(q_ref[rows, cols], keys) + bias
                s_sc[i, h] = s
                m_sc[h] = jnp.maximum(m_sc[h], jnp.maximum(s[:, :BLOCK], s[:, BLOCK:]))
            return 0

        lax.fori_loop(0, pairs, score, 0)
        for h in range(HEADS):
            m_sc[h] = jnp.broadcast_to(jnp.max(m_sc[h], axis=1, keepdims=True) * scale, (BLOCK, BLOCK))

        def weigh(i, _):
            e0, e1 = entries(i)
            for h in range(HEADS):
                cols = slice(h * HEAD, (h + 1) * HEAD)
                values = jnp.concatenate([v_ref[e0, :, cols], v_ref[e1, :, cols]], axis=0)
                s = s_sc[i, h]
                m = m_sc[h]
                p0 = jnp.exp2(s[:, :BLOCK] * scale - m)
                p1 = jnp.exp2(s[:, BLOCK:] * scale - m)
                l_sc[h] += p0 + p1
                p = jnp.concatenate([p0.astype(BF16), p1.astype(BF16)], axis=1)
                a_sc[h] += jnp.dot(p, values, preferred_element_type=F32)
            return 0

        lax.fori_loop(0, pairs, weigh, 0)
        for h in range(HEADS):
            total = jnp.sum(l_sc[h], axis=1, keepdims=True)
            att[rows, h * HEAD:(h + 1) * HEAD] = (a_sc[h] / total).astype(BF16)
        return 0

    lax.fori_loop(0, q_ref.shape[0] // BLOCK, block, 0)
    for c in range(0, o_ref.shape[1], 256):
        o_ref[:, c:c + 256] = jnp.dot(att[...], wo_ref[:, c:c + 256], preferred_element_type=F32).astype(BF16)


def attention(q, k, v, w_out, layout, counts):
    vmem = pl.BlockSpec(memory_space=pltpu.VMEM)
    smem = pl.BlockSpec(memory_space=pltpu.SMEM)
    pairs = layout.shape[1] // 2 + 1
    return pl.pallas_call(
        attention_kernel,
        out_shape=jax.ShapeDtypeStruct(q.shape, BF16),
        in_specs=[smem, smem, vmem, vmem, vmem, vmem],
        out_specs=vmem,
        scratch_shapes=[
            pltpu.VMEM((pairs, HEADS, BLOCK, 2 * BLOCK), F32),
            pltpu.VMEM((HEADS, BLOCK, BLOCK), F32),
            pltpu.VMEM((HEADS, BLOCK, BLOCK), F32),
            pltpu.VMEM((HEADS, BLOCK, HEAD), F32),
            pltpu.VMEM(q.shape, BF16),
        ],
        compiler_params=pltpu.CompilerParams(vmem_limit_bytes=56 << 20),
        name="attention",
    )(layout, counts, q, k, v, w_out)


def shards(normed, w_qkv, w_out, layout, counts):
    queries, keys, values, full_out = project_all(normed, w_qkv, w_out)
    shape = (-1, BLOCK, normed.shape[1])
    return attention(queries, keys.reshape(shape), values.reshape(shape), full_out, layout, counts)


def solution(mesh):
    return jax.shard_map(
        shards,
        mesh=mesh,
        in_specs=(
            P(("seq", "fsdp"), None),
            P("fsdp", None),
            P("fsdp", None),
            P(("seq", "fsdp"), None),
            P(("seq", "fsdp")),
        ),
        out_specs=P(("seq", "fsdp"), None),
        check_vma=False,
    )
```

time: 158 us -> 105 us (0.66)
  the two profiles are of different devices: /device:TPU:61 before, /device:TPU:1 now
where the time goes in v2:
time: 105 us; the launch traced here: 104 us
  Pallas kernels  99.2 us (94%)
  local copies, waits for them, and re-layouts  4.72 us (4%)
    pallas_call x1, Pallas kernels, project_all(): pl.pallas_call(project_kernel, out_shape=[jax.ShapeDtypeStruct((rows, wid...  67.9 us
    pallas_call x1, Pallas kernels, attention(): pl.pallas_call(attention_kernel, out_shape=jax.ShapeDtypeStruct(q.shape,...  31.3 us
    unnamed x8, local copies, waits for them, and re-layouts  4.72 us

profile of v2, /device:TPU:1, one launch (start us, length us, event | category | flops | bytes accessed | tf_op | source)
XLA Modules:
  0.0 103.9 jit_solution(16006323109914782094)
XLA Ops:
  0.0 0.0 copy-start.2
  0.0 1.1 %copy-done.2 = bf16[128,3072]{1,0:T(8,128)(2,1)S(1)} copy-done((bf16[128,3072]{1,0:T(8,128)(2,1)S(1)}, bf16[128,3072]{1,0:T(8,128)(2,1)}, u32[]{:S(2)}) %copy-start.2) | copy-done | bytes 786456
  1.1 0.0 copy-start.3
  1.1 0.9 copy-done.3
  2.1 67.9 %gather_and_project.1 = (bf16[1024,1024]{1,0:T(8,128)(2,1)S(1)}, bf16[3072,1024]{1,0:T(8,128)(2,1)}, bf16[3072,1024]{1,0:T(8,128)(2,1)}, bf16[1024,1024]{1,0:T(8,128)(2,1)S(1)}) custom-call(bf16[1024,1024]{1,0:T(8,128)(2,1)} %x.1, bf16[128,3072]{1,0:T(8,128)(2,1)S(1)} %copy-done.2, bf16[128,1024]{1,0:T(8,128)(2,1)S(1)} %copy-done.3), custom_call_target="tpu_custom_call" | custom-call | tf_op jit(solution)/shard_map/gather_and_project/pallas_call | solution.py:184
  70.0 0.0 copy-start
  70.0 1.3 %copy-done = bf16[1024,1024]{1,0:T(8,128)(2,1)} copy-done((bf16[1024,1024]{1,0:T(8,128)(2,1)}, bf16[1024,1024]{1,0:T(8,128)(2,1)S(1)}, u32[]{:S(2)}) %copy-start) | copy-done | bytes 2097176
  71.3 0.0 copy-start.1
  71.3 1.3 %copy-done.1 = bf16[1024,1024]{1,0:T(8,128)(2,1)} copy-done((bf16[1024,1024]{1,0:T(8,128)(2,1)}, bf16[1024,1024]{1,0:T(8,128)(2,1)S(1)}, u32[]{:S(2)}) %copy-start.1) | copy-done | bytes 2097176
  72.6 31.3 %attention.1 = bf16[1024,1024]{1,0:T(8,128)(2,1)} custom-call(s32[8,10]{1,0:T(8,128)} %layout.1, s32[8]{0:T(128)} %counts.1, bf16[1024,1024]{1,0:T(8,128)(2,1)} %copy-done, bf16[24,128,1024]{2,1,0:T(8,128)(2,1)} %bitcast.2, bf16[24,128,1024]{2,1,0:T(8,128)(2,1)} %bitcast.3, bf16[1024,1024]{1,0:T(8,128)(2,1)} %copy-done.1), custom_call_target="tpu_custom_call" | custom-call | tf_op jit(solution)/shard_map/attention/pallas_call | solution.py:274
Async XLA Ops:
  0.0 1.1 %copy-start.2 = (bf16[128,3072]{1,0:T(8,128)(2,1)S(1)}, bf16[128,3072]{1,0:T(8,128)(2,1)}, u32[]{:S(2)}) copy-start(bf16[128,3072]{1,0:T(8,128)(2,1)} %wq_shard.1) | copy-start | bytes 2359300
  1.1 0.9 copy-start.3
  70.0 1.3 %copy-start = (bf16[1024,1024]{1,0:T(8,128)(2,1)}, bf16[1024,1024]{1,0:T(8,128)(2,1)S(1)}, u32[]{:S(2)}) copy-start(bf16[1024,1024]{1,0:T(8,128)(2,1)S(1)} %get-tuple-element.9.q_ref) | copy-start | bytes 6291460
  71.3 1.3 %copy-start.1 = (bf16[1024,1024]{1,0:T(8,128)(2,1)}, bf16[1024,1024]{1,0:T(8,128)(2,1)S(1)}, u32[]{:S(2)}) copy-start(bf16[1024,1024]{1,0:T(8,128)(2,1)S(1)} %get-tuple-element.12.wo_ref) | copy-start | bytes 6291460

commit v3 on v2

v3 whole, which is shorter than its diff:
```python
import functools

import jax
import jax.numpy as jnp
from jax import lax
from jax.experimental import pallas as pl
from jax.experimental.pallas import tpu as pltpu
from jax.sharding import PartitionSpec as P

HEADS = 8
BLOCK = 128
HEAD = 128
MESH = pl.DeviceIdType.MESH
LOG2E = 1.4426950408889634
NEG = float("-inf")
F32 = jnp.float32
BF16 = jnp.bfloat16


def over_sublanes(value, op):
    result = value[:8]
    for i in range(8, value.shape[0], 8):
        result = op(result, value[i:i + 8])
    return result


def attend_block(layout, counts, b, q_sc, k_sc, vt_sc, score_refs, att):
    scale = HEAD ** -0.5 * LOG2E
    slots = layout.shape[1] + 1
    blocks = q_sc.shape[0]
    pair = 2 * HEAD
    pairs = HEADS // 2
    entry = [blocks + b] + [layout[b, j] for j in range(slots - 1)]
    used = counts[b]
    rows = pl.ds(pl.multiple_of(b * BLOCK, BLOCK), BLOCK)
    zero = jnp.zeros((HEAD, BLOCK), BF16)
    largest = [None] * pairs
    for g in range(-1, pairs):
        ahead = g + 1
        scoring, weighing = ahead < pairs, g >= 0
        if scoring:
            cols = slice(ahead * pair, (ahead + 1) * pair)
            q0 = q_sc[b, :, ahead * pair:ahead * pair + HEAD]
            q1 = q_sc[b, :, ahead * pair + HEAD:(ahead + 1) * pair]
            q_pair = jnp.concatenate(
                [jnp.concatenate([q0.T, zero], 1), jnp.concatenate([zero, q1.T], 1)], 0)
            top = None
        if weighing:
            total = None
            summed = [None, None]
            held = []

        def apply_values():
            for h in range(2):
                head = slice(g * pair + h * HEAD, g * pair + (h + 1) * HEAD)
                left = [vt_sc[entry[i], head, :] for i, _ in held]
                right = [p[:, h * BLOCK:(h + 1) * BLOCK] for _, p in held]
                if len(held) > 1:
                    left, right = [jnp.concatenate(left, 1)], [jnp.concatenate(right, 0)]
                term = jnp.dot(left[0], right[0], preferred_element_type=F32)
                summed[h] = term if summed[h] is None else summed[h] + term
            held.clear()

        for i in range(slots):
            if scoring:
                scores = jnp.dot(k_sc[entry[i], :, cols], q_pair, preferred_element_type=F32)
            if weighing:
                if len(held) == 2:
                    apply_values()
                p = jnp.exp2(score_refs[g % 2][i] * scale - largest[g])
                part = over_sublanes(p, jnp.add)
                total = part if total is None else total + part
                held.append((i, p.astype(BF16)))
            if scoring:
                if i > 1:
                    scores = scores + jnp.where(i <= used, 0.0, NEG)
                score_refs[ahead % 2][i] = scores
                part = over_sublanes(scores, jnp.maximum)
                top = part if top is None else jnp.maximum(top, part)
        if weighing:
            apply_values()
            inverse = 1.0 / jnp.sum(total, axis=0, keepdims=True)
            for h in range(2):
                head = slice(g * pair + h * HEAD, g * pair + (h + 1) * HEAD)
                att[rows, head] = (summed[h] * inverse[:, h * BLOCK:(h + 1) * BLOCK]).T.astype(BF16)
        if scoring:
            largest[ahead] = jnp.max(top, axis=0, keepdims=True) * scale


def sublayer_kernel(layout, counts, x_hbm, wq_shard, wo_shard, out, x, wq, wo, inner, outer, q_sc, k_sc, vt_sc, s0_sc,
                    s1_sc, att, send, recv, send2, recv2, own, x_send, x_recv):
    s = lax.axis_index("seq")
    f = lax.axis_index("fsdp")
    count = lax.axis_size("seq")
    core = lax.rem(s, 2)
    side = 2 * core - 1
    mate = (s - side, f)
    beyond = (lax.rem(s + side + count, count), f)
    y = lax.rem(f, 2)
    z = f // 2
    fy = 2 * z + 1 - y
    s_flip = s + 2 - 4 * lax.rem(s // 2, 2)
    up, down, far = lax.rem(z + 1, 4), lax.rem(z + 3, 4), lax.rem(z + 2, 4)
    dev_y, dev_y2, dev_up, dev_down = (s, fy), (s_flip, fy), (s, 2 * up + y), (s, 2 * down + y)
    barrier = pltpu.get_barrier_semaphore()
    for peer in (dev_y, dev_y2, dev_up, dev_down, mate, beyond):
        pl.semaphore_signal(barrier, inc=1, device_id=peer, device_id_type=MESH)
    pl.semaphore_wait(barrier, 6)
    rows = wq_shard.shape[0]
    half = rows // 2
    quarter = rows // 4
    arrays = ((wq_shard, wq), (wo_shard, wo))
    pending = []

    def start(copy):
        copy.start()
        return copy

    def part(owner, offset, size):
        return pl.ds(pl.multiple_of(owner * rows + core * half + offset, quarter), size)

    def send_to(a, k, owner, offset, size, peer, local):
        shard, full = arrays[a]
        place = part(owner, offset, size)
        source = shard.at[pl.ds(pl.multiple_of(core * half + offset, quarter), size)] if local else full.at[place]
        copy = start(pltpu.make_async_remote_copy(
            source, full.at[place], send.at[a, k], recv.at[a, k], device_id=peer, device_id_type=MESH))
        pending.append(copy)
        return copy

    def hand(a, k, owner):
        full = arrays[a][1]
        place = part(owner, 0, half)
        return start(pltpu.make_async_remote_copy(
            full.at[place], full.at[place], send2.at[a, k], recv2.at[a, k], device_id=mate, device_id_type=MESH))

    def send_y(a):
        return (send_to(a, 0, f, 0, quarter, dev_y, True), send_to(a, 9, f, quarter, quarter, dev_y2, True))

    def send_own(a):
        return (send_to(a, 1, f, 0, half, dev_up, True), send_to(a, 2, f, 0, half, dev_down, True))

    def send_other(a):
        return (send_to(a, 3, fy, 0, half, dev_up, False), send_to(a, 4, fy, 0, half, dev_down, False))

    def onward(a, first, odd):
        lane = 1 - y if odd else y
        k = 7 if odd else 5
        h = 3 if odd else 1
        first[0].wait_recv()
        c_up = send_to(a, k, 2 * down + lane, 0, quarter, dev_up, False)
        h_up = hand(a, h, 2 * down + lane)
        first[1].wait_recv()
        c_down = send_to(a, k + 1, 2 * up + lane, quarter, quarter, dev_down, False)
        return (c_up, c_down), [h_up, hand(a, h + 1, 2 * up + lane)]

    def last(a, second, odd):
        second[0].wait_recv()
        second[1].wait_recv()
        return [hand(a, 6 if odd else 5, 2 * far + (1 - y if odd else y))]

    x_copy = start(pltpu.make_async_copy(x_hbm, x, own.at[2]))
    y_q = send_y(0)
    own_q = send_own(0)
    place = pl.ds(pl.multiple_of(f * rows, rows), rows)
    own_copy_q, own_copy_o = [
        start(pltpu.make_async_copy(shard, full.at[place], own.at[a])) for a, (shard, full) in enumerate(arrays)]
    y_o = send_y(1)
    inner_copy = start(pltpu.make_async_remote_copy(
        x_hbm, inner, x_send.at[8], x_recv.at[8], device_id=mate, device_id_type=MESH))
    for copy in y_q:
        copy.wait_recv()
    other_q = send_other(0)
    hands_q = [hand(0, 0, fy)]
    step = x.shape[0] // 8
    outer_copies = []
    for i in range(8):
        place = pl.ds(i * step, step)
        outer_copies.append(start(pltpu.make_async_remote_copy(
            x_hbm.at[place], outer.at[place], x_send.at[i], x_recv.at[i], device_id=beyond, device_id_type=MESH)))
    onward_q, more = onward(0, own_q, False)
    hands_q += more
    onward_q2, more = onward(0, other_q, True)
    hands_q += more
    own_o = send_own(1)
    for copy in y_o:
        copy.wait_recv()
    other_o = send_other(1)
    hands_o = [hand(1, 0, fy)]
    hands_q += last(0, onward_q, False)
    hands_q += last(0, onward_q2, True)
    own_copy_q.wait()
    for copy in hands_q:
        copy.wait_recv()

    x_copy.wait()
    width = x.shape[1]
    tile = 256
    total = x.shape[0]
    blocks = total // BLOCK

    def project(source, target, first, offset):
        def one(n, _):
            w_cols = pl.ds(pl.multiple_of(offset + n * tile, tile), tile)
            value = jnp.dot(source[...], wq[:, w_cols], preferred_element_type=F32).astype(BF16)
            cols = pl.ds(pl.multiple_of(n * tile, tile), tile)
            for j in range(value.shape[0] // BLOCK):
                piece = value[j * BLOCK:(j + 1) * BLOCK]
                if offset == 2 * width:
                    target[first + j, cols, :] = piece.T
                else:
                    target[first + j, :, cols] = piece
            return 0

        lax.fori_loop(0, width // tile, one, 0)

    project(x, q_sc, 0, 0)
    onward_o, more = onward(1, own_o, False)
    hands_o += more
    project(x, k_sc, blocks, width)
    project(x, vt_sc, blocks, 2 * width)
    onward_o2, more = onward(1, other_o, True)
    hands_o += more
    inner_copy.wait_recv()
    inner_first = (1 - core) * 2 * blocks
    project(inner, k_sc, inner_first, width)
    project(inner, vt_sc, inner_first, 2 * width)
    hands_o += last(1, onward_o, False)
    hands_o += last(1, onward_o2, True)
    pieces = 4
    size = total // pieces
    for i in range(pieces):
        for copy in outer_copies[i * 8 // pieces:(i + 1) * 8 // pieces]:
            copy.wait_recv()
        piece = outer.at[pl.ds(i * size, size)]
        first = core * 2 * blocks + i * (size // BLOCK)
        project(piece, k_sc, first, width)
        project(piece, vt_sc, first, 2 * width)

    def block(b, _):
        attend_block(layout, counts, b, q_sc, k_sc, vt_sc, (s0_sc, s1_sc), att)
        return 0

    lax.fori_loop(0, blocks, block, 0)
    own_copy_o.wait()
    for copy in hands_o:
        copy.wait_recv()
    for c in range(0, width, tile):
        out[:, c:c + tile] = jnp.dot(att[...], wo[:, c:c + tile], preferred_element_type=F32).astype(BF16)
    for copy in pending + hands_q + hands_o + outer_copies + [inner_copy]:
        copy.wait_send()


def shards(normed, w_qkv, w_out, layout, counts):
    hbm = pl.BlockSpec(memory_space=pl.ANY)
    smem = pl.BlockSpec(memory_space=pltpu.SMEM)
    vmem = pl.BlockSpec(memory_space=pltpu.VMEM)
    dma = pltpu.SemaphoreType.DMA
    rows, width = normed.shape
    blocks = rows // BLOCK
    slots = layout.shape[1] + 1
    return pl.pallas_call(
        sublayer_kernel,
        out_shape=jax.ShapeDtypeStruct((rows, width), BF16),
        in_specs=[smem, smem, hbm, hbm, hbm],
        out_specs=vmem,
        scratch_shapes=[
            pltpu.VMEM((rows, width), BF16),
            pltpu.VMEM((8 * w_qkv.shape[0], w_qkv.shape[1]), BF16),
            pltpu.VMEM((8 * w_out.shape[0], w_out.shape[1]), BF16),
            pltpu.VMEM((rows, width), BF16),
            pltpu.VMEM((rows, width), BF16),
            pltpu.VMEM((blocks, BLOCK, width), BF16),
            pltpu.VMEM((3 * blocks, BLOCK, width), BF16),
            pltpu.VMEM((3 * blocks, width, BLOCK), BF16),
            pltpu.VMEM((slots, BLOCK, 2 * HEAD), F32),
            pltpu.VMEM((slots, BLOCK, 2 * HEAD), F32),
            pltpu.VMEM((rows, width), BF16),
            dma((2, 10)), dma((2, 10)), dma((2, 7)), dma((2, 7)), dma((3,)), dma((9,)), dma((9,)),
        ],
        compiler_params=pltpu.CompilerParams(
            collective_id=0, has_side_effects=True, vmem_limit_bytes=60 << 20),
        name="sublayer",
    )(layout, counts, normed, w_qkv, w_out)


def solution(mesh):
    return jax.shard_map(
        shards,
        mesh=mesh,
        in_specs=(
            P(("seq", "fsdp"), None),
            P("fsdp", None),
            P("fsdp", None),
            P(("seq", "fsdp"), None),
            P(("seq", "fsdp")),
        ),
        out_specs=P(("seq", "fsdp"), None),
        check_vma=False,
    )
```

time: 105 us -> 104 us (level)
  the two profiles are of different devices: /device:TPU:1 before, /device:TPU:19 now
where the time goes in v3:
time: 104 us
  Pallas kernels  101 us (97%)
  local copies, waits for them, and re-layouts  3.08 us (3%)
    pallas_call x1, Pallas kernels, shards(): pl.pallas_call(sublayer_kernel, out_shape=jax.ShapeDtypeStruct((rows, wid...  101 us
    unnamed x1, local copies, waits for them, and re-layouts  3.08 us

profile of v3, /device:TPU:19, one launch (start us, length us, event | category | flops | bytes accessed | tf_op | source)
XLA Modules:
  0.0 103.7 jit_solution(16036474096190427287)
XLA Ops:
  0.0 100.6 %sublayer.1 = bf16[1024,1024]{1,0:T(8,128)(2,1)} custom-call(s32[8,10]{1,0:T(8,128)} %layout.1, s32[8]{0:T(128)} %counts.1, bf16[1024,1024]{1,0:T(8,128)(2,1)} %x_hbm.1, bf16[128,3072]{1,0:T(8,128)(2,1)} %wq_shard.1, bf16[128,1024]{1,0:T(8,128)(2,1)} %wo_shard.1), custom_call_target="tpu_custom_call" | custom-call | tf_op jit(solution)/shard_map/sublayer/pallas_call | solution.py:262
  100.6 3.1 %copy.7 = bf16[1024,1024]{1,0:T(8,128)(2,1)} copy(bf16[1024,1024]{1,0:T(8,128)(2,1)} %sublayer.1) | data formatting | bytes 4194304

commit v4 on v3

--- a/solution.py
+++ b/solution.py
@@ -24,71 +24,74 @@
     return result
 
 
-def attend_block(layout, counts, b, q_sc, k_sc, vt_sc, score_refs, att):
-    scale = HEAD ** -0.5 * LOG2E
+def score_and_weigh(layout, counts, scored, weighed, q_sc, k_sc, vt_sc, score_refs, top_sc, att):
     slots = layout.shape[1] + 1
     blocks = q_sc.shape[0]
     pair = 2 * HEAD
-    pairs = HEADS // 2
-    entry = [blocks + b] + [layout[b, j] for j in range(slots - 1)]
-    used = counts[b]
-    rows = pl.ds(pl.multiple_of(b * BLOCK, BLOCK), BLOCK)
     zero = jnp.zeros((HEAD, BLOCK), BF16)
-    largest = [None] * pairs
-    for g in range(-1, pairs):
-        ahead = g + 1
-        scoring, weighing = ahead < pairs, g >= 0
-        if scoring:
-            cols = slice(ahead * pair, (ahead + 1) * pair)
-            q0 = q_sc[b, :, ahead * pair:ahead * pair + HEAD]
-            q1 = q_sc[b, :, ahead * pair + HEAD:(ahead + 1) * pair]
-            q_pair = jnp.concatenate(
-                [jnp.concatenate([q0.T, zero], 1), jnp.concatenate([zero, q1.T], 1)], 0)
-            top = None
-        if weighing:
-            total = None
-            summed = [None, None]
-            held = []
-
-        def apply_values():
-            for h in range(2):
-                head = slice(g * pair + h * HEAD, g * pair + (h + 1) * HEAD)
-                left = [vt_sc[entry[i], head, :] for i, _ in held]
-                right = [p[:, h * BLOCK:(h + 1) * BLOCK] for _, p in held]
-                if len(held) > 1:
-                    left, right = [jnp.concatenate(left, 1)], [jnp.concatenate(right, 0)]
-                term = jnp.dot(left[0], right[0], preferred_element_type=F32)
-                summed[h] = term if summed[h] is None else summed[h] + term
-            held.clear()
-
-        for i in range(slots):
-            if scoring:
-                scores = jnp.dot(k_sc[entry[i], :, cols], q_pair, preferred_element_type=F32)
-            if weighing:
-                if len(held) == 2:
-                    apply_values()
-                p = jnp.exp2(score_refs[g % 2][i] * scale - largest[g])
-                part = over_sublanes(p, jnp.add)
-                total = part if total is None else total + part
-                held.append((i, p.astype(BF16)))
-            if scoring:
-                if i > 1:
-                    scores = scores + jnp.where(i <= used, 0.0, NEG)
-                score_refs[ahead % 2][i] = scores
-                part = over_sublanes(scores, jnp.maximum)
-                top = part if top is None else jnp.maximum(top, part)
-        if weighing:
-            apply_values()
-            inverse = 1.0 / jnp.sum(total, axis=0, keepdims=True)
-            for h in range(2):
-                head = slice(g * pair + h * HEAD, g * pair + (h + 1) * HEAD)
-                att[rows, head] = (summed[h] * inverse[:, h * BLOCK:(h + 1) * BLOCK]).T.astype(BF16)
-        if scoring:
-            largest[ahead] = jnp.max(top, axis=0, keepdims=True) * scale
+
+    def entries(b):
+        return [blocks + b] + [layout[b, j] for j in range(slots - 1)]
+
+    if scored is not None:
+        b, g, buffer = scored
+        entry = entries(b)
+        used = counts[b]
+        q0 = q_sc[b, :, g * pair:g * pair + HEAD]
+        q1 = q_sc[b, :, g * pair + HEAD:(g + 1) * pair]
+        q_pair = jnp.concatenate([jnp.concatenate([q0.T, zero], 1), jnp.concatenate([zero, q1.T], 1)], 0)
+        top = None
+    if weighed is not None:
+        b2, g2, buffer2 = weighed
+        entry2 = entries(b2)
+        largest = top_sc[buffer2]
+        largest = largest[0:1]
+        total = None
+        summed = [None, None]
+        held = []
+
+    def head_rows(h):
+        return slice(g2 * pair + h * HEAD, g2 * pair + (h + 1) * HEAD)
+
+    def apply_values():
+        for h in range(2):
+            left = [vt_sc[entry2[i], head_rows(h), :] for i, _ in held]
+            right = [p[:, h * BLOCK:(h + 1) * BLOCK] for _, p in held]
+            if len(held) > 1:
+                left, right = [jnp.concatenate(left, 1)], [jnp.concatenate(right, 0)]
+            term = jnp.dot(left[0], right[0], preferred_element_type=F32)
+            summed[h] = term if summed[h] is None else summed[h] + term
+        held.clear()
+
+    for i in range(slots):
+        if scored is not None:
+            scores = jnp.dot(
+                k_sc[entry[i], :, g * pair:(g + 1) * pair], q_pair, preferred_element_type=F32)
+        if weighed is not None:
+            if len(held) == 2:
+                apply_values()
+            p = jnp.exp2(score_refs[buffer2][i] - largest)
+            part = over_sublanes(p, jnp.add)
+            total = part if total is None else total + part
+            held.append((i, p.astype(BF16)))
+        if scored is not None:
+            if i > 1:
+                scores = scores + jnp.where(i <= used, 0.0, NEG)
+            score_refs[buffer][i] = scores
+            part = over_sublanes(scores, jnp.maximum)
+            top = part if top is None else jnp.maximum(top, part)
+    if weighed is not None:
+        apply_values()
+        inverse = 1.0 / jnp.sum(total, axis=0, keepdims=True)
+        rows = pl.ds(pl.multiple_of(b2 * BLOCK, BLOCK), BLOCK)
+        for h in range(2):
+            att[rows, head_rows(h)] = (summed[h] * inverse[:, h * BLOCK:(h + 1) * BLOCK]).T.astype(BF16)
+    if scored is not None:
+        top_sc[buffer] = jnp.broadcast_to(jnp.max(top, axis=0, keepdims=True), top.shape)
 
 
 def sublayer_kernel(layout, counts, x_hbm, wq_shard, wo_shard, out, x, wq, wo, inner, outer, q_sc, k_sc, vt_sc, s0_sc,
-                    s1_sc, att, send, recv, send2, recv2, own, x_send, x_recv):
+                    s1_sc, top_sc, att, send, recv, send2, recv2, own, x_send, x_recv):
     s = lax.axis_index("seq")
     f = lax.axis_index("fsdp")
     count = lax.axis_size("seq")
@@ -101,14 +104,20 @@
     fy = 2 * z + 1 - y
     s_flip = s + 2 - 4 * lax.rem(s // 2, 2)
     up, down, far = lax.rem(z + 1, 4), lax.rem(z + 3, 4), lax.rem(z + 2, 4)
-    dev_y, dev_y2, dev_up, dev_down = (s, fy), (s_flip, fy), (s, 2 * up + y), (s, 2 * down + y)
+    dev_y = (jnp.where(core == 0, s, s_flip), fy)
+    dev_up, dev_down = (s, 2 * up + y), (s, 2 * down + y)
+    x_count = 4
+    stride = count // x_count
+    x_pos = s // stride
+    along_x = [(lax.rem(s + k * stride, count), f) for k in range(1, x_count)]
     barrier = pltpu.get_barrier_semaphore()
-    for peer in (dev_y, dev_y2, dev_up, dev_down, mate, beyond):
+    for peer in [dev_y, dev_up, dev_down, mate, beyond] + along_x:
         pl.semaphore_signal(barrier, inc=1, device_id=peer, device_id_type=MESH)
-    pl.semaphore_wait(barrier, 6)
+    pl.semaphore_wait(barrier, 5 + len(along_x))
     rows = wq_shard.shape[0]
     half = rows // 2
     quarter = rows // 4
+    slice_rows = half // x_count
     arrays = ((wq_shard, wq), (wo_shard, wo))
     pending = []
 
@@ -117,12 +126,12 @@
         return copy
 
     def part(owner, offset, size):
-        return pl.ds(pl.multiple_of(owner * rows + core * half + offset, quarter), size)
+        return pl.ds(pl.multiple_of(owner * rows + core * half + offset, slice_rows), size)
 
     def send_to(a, k, owner, offset, size, peer, local):
         shard, full = arrays[a]
         place = part(owner, offset, size)
-        source = shard.at[pl.ds(pl.multiple_of(core * half + offset, quarter), size)] if local else full.at[place]
+        source = shard.at[pl.ds(pl.multiple_of(core * half + offset, slice_rows), size)] if local else full.at[place]
         copy = start(pltpu.make_async_remote_copy(
             source, full.at[place], send.at[a, k], recv.at[a, k], device_id=peer, device_id_type=MESH))
         pending.append(copy)
@@ -135,7 +144,11 @@
             full.at[place], full.at[place], send2.at[a, k], recv2.at[a, k], device_id=mate, device_id_type=MESH))
 
     def send_y(a):
-        return (send_to(a, 0, f, 0, quarter, dev_y, True), send_to(a, 9, f, quarter, quarter, dev_y2, True))
+        return send_to(a, 0, f, x_pos * slice_rows, slice_rows, dev_y, True)
+
+    def spread(a, first):
+        first.wait_recv()
+        return [send_to(a, 9 + k, fy, x_pos * slice_rows, slice_rows, peer, False) for k, peer in enumerate(along_x)]
 
     def send_own(a):
         return (send_to(a, 1, f, 0, half, dev_up, True), send_to(a, 2, f, 0, half, dev_down, True))
@@ -168,27 +181,29 @@
     y_o = send_y(1)
     inner_copy = start(pltpu.make_async_remote_copy(
         x_hbm, inner, x_send.at[8], x_recv.at[8], device_id=mate, device_id_type=MESH))
-    for copy in y_q:
-        copy.wait_recv()
-    other_q = send_other(0)
-    hands_q = [hand(0, 0, fy)]
+    spread_q = spread(0, y_q)
     step = x.shape[0] // 8
     outer_copies = []
     for i in range(8):
         place = pl.ds(i * step, step)
         outer_copies.append(start(pltpu.make_async_remote_copy(
             x_hbm.at[place], outer.at[place], x_send.at[i], x_recv.at[i], device_id=beyond, device_id_type=MESH)))
+    for copy in spread_q:
+        copy.wait_recv()
+    other_q = send_other(0)
+    hands_q = [hand(0, 0, fy)]
     onward_q, more = onward(0, own_q, False)
     hands_q += more
     onward_q2, more = onward(0, other_q, True)
     hands_q += more
+    hands_q += last(0, onward_q, False)
+    hands_q += last(0, onward_q2, True)
+    spread_o = spread(1, y_o)
     own_o = send_own(1)
-    for copy in y_o:
+    for copy in spread_o:
         copy.wait_recv()
     other_o = send_other(1)
     hands_o = [hand(1, 0, fy)]
-    hands_q += last(0, onward_q, False)
-    hands_q += last(0, onward_q2, True)
     own_copy_q.wait()
     for copy in hands_q:
         copy.wait_recv()
@@ -202,7 +217,10 @@
     def project(source, target, first, offset):
         def one(n, _):
             w_cols = pl.ds(pl.multiple_of(offset + n * tile, tile), tile)
-            value = jnp.dot(source[...], wq[:, w_cols], preferred_element_type=F32).astype(BF16)
+            value = jnp.dot(source[...], wq[:, w_cols], preferred_element_type=F32)
+            if offset == 0:
+                value = value * (HEAD ** -0.5 * LOG2E)
+            value = value.astype(BF16)
             cols = pl.ds(pl.multiple_of(n * tile, tile), tile)
             for j in range(value.shape[0] // BLOCK):
                 piece = value[j * BLOCK:(j + 1) * BLOCK]
@@ -237,10 +255,18 @@
         project(piece, k_sc, first, width)
         project(piece, vt_sc, first, 2 * width)
 
+    def step(scored, weighed):
+        score_and_weigh(layout, counts, scored, weighed, q_sc, k_sc, vt_sc, (s0_sc, s1_sc), top_sc, att)
+
+    pairs = HEADS // 2
+
     def block(b, _):
-        attend_block(layout, counts, b, q_sc, k_sc, vt_sc, (s0_sc, s1_sc), att)
+        for g in range(pairs):
+            following = (b, g + 1) if g + 1 < pairs else (jnp.minimum(b + 1, blocks - 1), 0)
+            step(following + ((g + 1) % 2,), (b, g, g % 2))
         return 0
 
+    step((0, 0, 0), None)
     lax.fori_loop(0, blocks, block, 0)
     own_copy_o.wait()
     for copy in hands_o:
@@ -275,8 +301,9 @@
             pltpu.VMEM((3 * blocks, width, BLOCK), BF16),
             pltpu.VMEM((slots, BLOCK, 2 * HEAD), F32),
             pltpu.VMEM((slots, BLOCK, 2 * HEAD), F32),
+            pltpu.VMEM((2, 8, 2 * HEAD), F32),
             pltpu.VMEM((rows, width), BF16),
-            dma((2, 10)), dma((2, 10)), dma((2, 7)), dma((2, 7)), dma((3,)), dma((9,)), dma((9,)),
+            dma((2, 12)), dma((2, 12)), dma((2, 7)), dma((2, 7)), dma((3,)), dma((9,)), dma((9,)),
         ],
         compiler_params=pltpu.CompilerParams(
             collective_id=0, has_side_effects=True, vmem_limit_bytes=60 << 20),

time: 104 us -> 95 us (0.913)
  the two profiles are of different devices: /device:TPU:19 before, /device:TPU:1 now
where the time goes in v4:
time: 95 us; the launch traced here: 94.8 us
  Pallas kernels  91.7 us (97%)
  local copies, waits for them, and re-layouts  3.08 us (3%)
    pallas_call x1, Pallas kernels, shards(): pl.pallas_call(sublayer_kernel, out_shape=jax.ShapeDtypeStruct((rows, wid...  91.7 us
    unnamed x1, local copies, waits for them, and re-layouts  3.08 us

profile of v4, /device:TPU:1, one launch (start us, length us, event | category | flops | bytes accessed | tf_op | source)
XLA Modules:
  0.0 94.8 jit_solution(6165221463181901739)
XLA Ops:
  0.0 91.7 %sublayer.1 = bf16[1024,1024]{1,0:T(8,128)(2,1)} custom-call(s32[8,10]{1,0:T(8,128)} %layout.1, s32[8]{0:T(128)} %counts.1, bf16[1024,1024]{1,0:T(8,128)(2,1)} %x_hbm.1, bf16[128,3072]{1,0:T(8,128)(2,1)} %wq_shard.1, bf16[128,1024]{1,0:T(8,128)(2,1)} %wo_shard.1), custom_call_target="tpu_custom_call" | custom-call | tf_op jit(solution)/shard_map/sublayer/pallas_call | solution.py:288
  91.8 3.1 %copy.7 = bf16[1024,1024]{1,0:T(8,128)(2,1)} copy(bf16[1024,1024]{1,0:T(8,128)(2,1)} %sublayer.1) | data formatting | bytes 4194304

commit v5 on v4

--- a/solution.py
+++ b/solution.py
@@ -25,6 +25,7 @@
 
 
 def score_and_weigh(layout, counts, scored, weighed, q_sc, k_sc, vt_sc, score_refs, top_sc, att):
+    scale = HEAD ** -0.5 * LOG2E
     slots = layout.shape[1] + 1
     blocks = q_sc.shape[0]
     pair = 2 * HEAD
@@ -70,7 +71,7 @@
         if weighed is not None:
             if len(held) == 2:
                 apply_values()
-            p = jnp.exp2(score_refs[buffer2][i] - largest)
+            p = jnp.exp2(score_refs[buffer2][i] * scale - largest)
             part = over_sublanes(p, jnp.add)
             total = part if total is None else total + part
             held.append((i, p.astype(BF16)))
@@ -87,11 +88,11 @@
         for h in range(2):
             att[rows, head_rows(h)] = (summed[h] * inverse[:, h * BLOCK:(h + 1) * BLOCK]).T.astype(BF16)
     if scored is not None:
-        top_sc[buffer] = jnp.broadcast_to(jnp.max(top, axis=0, keepdims=True), top.shape)
+        top_sc[buffer] = jnp.broadcast_to(jnp.max(top, axis=0, keepdims=True) * scale, top.shape)
 
 
 def sublayer_kernel(layout, counts, x_hbm, wq_shard, wo_shard, out, x, wq, wo, inner, outer, q_sc, k_sc, vt_sc, s0_sc,
-                    s1_sc, top_sc, att, send, recv, send2, recv2, own, x_send, x_recv):
+                    s1_sc, top_sc, att, own_sums, inner_sums, send, recv, send2, recv2, own, x_send, x_recv):
     s = lax.axis_index("seq")
     f = lax.axis_index("fsdp")
     count = lax.axis_size("seq")
@@ -192,34 +193,38 @@
         copy.wait_recv()
     other_q = send_other(0)
     hands_q = [hand(0, 0, fy)]
+    spread_o = spread(1, y_o)
     onward_q, more = onward(0, own_q, False)
     hands_q += more
     onward_q2, more = onward(0, other_q, True)
     hands_q += more
-    hands_q += last(0, onward_q, False)
-    hands_q += last(0, onward_q2, True)
-    spread_o = spread(1, y_o)
-    own_o = send_own(1)
-    for copy in spread_o:
-        copy.wait_recv()
-    other_o = send_other(1)
-    hands_o = [hand(1, 0, fy)]
-    own_copy_q.wait()
-    for copy in hands_q:
-        copy.wait_recv()
-
-    x_copy.wait()
     width = x.shape[1]
     tile = 256
     total = x.shape[0]
     blocks = total // BLOCK
 
-    def project(source, target, first, offset):
+    early = [pl.ds(pl.multiple_of(2 * pair * rows, 2 * rows), 2 * rows) for pair in (z, up, down)]
+    late = pl.ds(pl.multiple_of(2 * far * rows, 2 * rows), 2 * rows)
+
+    def begin(source, sums, offset, base=0):
         def one(n, _):
             w_cols = pl.ds(pl.multiple_of(offset + n * tile, tile), tile)
-            value = jnp.dot(source[...], wq[:, w_cols], preferred_element_type=F32)
-            if offset == 0:
-                value = value * (HEAD ** -0.5 * LOG2E)
+            s_cols = pl.ds(pl.multiple_of(offset - base + n * tile, tile), tile)
+            terms = [
+                jnp.dot(source[:, part_rows], wq[part_rows, w_cols], preferred_element_type=F32) for part_rows in early]
+            sums[:, s_cols] = terms[0] + terms[1] + terms[2]
+            return 0
+
+        lax.fori_loop(0, width // tile, one, 0)
+
+    def project(source, target, first, offset, sums=None, base=0):
+        def one(n, _):
+            w_cols = pl.ds(pl.multiple_of(offset + n * tile, tile), tile)
+            if sums is None:
+                value = jnp.dot(source[...], wq[:, w_cols], preferred_element_type=F32)
+            else:
+                s_cols = pl.ds(pl.multiple_of(offset - base + n * tile, tile), tile)
+                value = sums[:, s_cols] + jnp.dot(source[:, late], wq[late, w_cols], preferred_element_type=F32)
             value = value.astype(BF16)
             cols = pl.ds(pl.multiple_of(n * tile, tile), tile)
             for j in range(value.shape[0] // BLOCK):
@@ -232,17 +237,34 @@
 
         lax.fori_loop(0, width // tile, one, 0)
 
-    project(x, q_sc, 0, 0)
+    x_copy.wait()
+    own_copy_q.wait()
+    for copy in hands_q:
+        copy.wait_recv()
+    for third in range(3):
+        begin(x, own_sums, third * width)
+    last_hands = last(0, onward_q, False) + last(0, onward_q2, True)
+    hands_q += last_hands
+    own_o = send_own(1)
+    for copy in spread_o:
+        copy.wait_recv()
+    other_o = send_other(1)
+    hands_o = [hand(1, 0, fy)]
+    inner_copy.wait_recv()
+    for third in (1, 2):
+        begin(inner, inner_sums, third * width, width)
+    for copy in last_hands:
+        copy.wait_recv()
+    project(x, q_sc, 0, 0, own_sums)
+    project(x, k_sc, blocks, width, own_sums)
     onward_o, more = onward(1, own_o, False)
     hands_o += more
-    project(x, k_sc, blocks, width)
-    project(x, vt_sc, blocks, 2 * width)
+    project(x, vt_sc, blocks, 2 * width, own_sums)
+    inner_first = (1 - core) * 2 * blocks
+    project(inner, k_sc, inner_first, width, inner_sums, width)
     onward_o2, more = onward(1, other_o, True)
     hands_o += more
-    inner_copy.wait_recv()
-    inner_first = (1 - core) * 2 * blocks
-    project(inner, k_sc, inner_first, width)
-    project(inner, vt_sc, inner_first, 2 * width)
+    project(inner, vt_sc, inner_first, 2 * width, inner_sums, width)
     hands_o += last(1, onward_o, False)
     hands_o += last(1, onward_o2, True)
     pieces = 4
@@ -303,6 +325,8 @@
             pltpu.VMEM((slots, BLOCK, 2 * HEAD), F32),
             pltpu.VMEM((2, 8, 2 * HEAD), F32),
             pltpu.VMEM((rows, width), BF16),
+            pltpu.VMEM((rows, 3 * width), F32),
+            pltpu.VMEM((rows, 2 * width), F32),
             dma((2, 12)), dma((2, 12)), dma((2, 7)), dma((2, 7)), dma((3,)), dma((9,)), dma((9,)),
         ],
         compiler_params=pltpu.CompilerParams(

time: 95 us -> 93.7 us (0.986)
  the two profiles are of different devices: /device:TPU:1 before, /device:TPU:0 now
where the time goes in v5:
time: 93.7 us; the launch traced here: 93.6 us
  Pallas kernels  90.5 us (97%)
  local copies, waits for them, and re-layouts  3.08 us (3%)
    pallas_call x1, Pallas kernels, shards(): pl.pallas_call(sublayer_kernel, out_shape=jax.ShapeDtypeStruct((rows, wid...  90.5 us
    unnamed x1, local copies, waits for them, and re-layouts  3.08 us

profile of v5, /device:TPU:0, one launch (start us, length us, event | category | flops | bytes accessed | tf_op | source)
XLA Modules:
  0.0 93.6 jit_solution(17698572443262775572)
XLA Ops:
  0.0 90.5 %sublayer.1 = bf16[1024,1024]{1,0:T(8,128)(2,1)} custom-call(s32[8,10]{1,0:T(8,128)} %layout.1, s32[8]{0:T(128)} %counts.1, bf16[1024,1024]{1,0:T(8,128)(2,1)} %x_hbm.1, bf16[128,3072]{1,0:T(8,128)(2,1)} %wq_shard.1, bf16[128,1024]{1,0:T(8,128)(2,1)} %wo_shard.1), custom_call_target="tpu_custom_call" | custom-call | tf_op jit(solution)/shard_map/sublayer/pallas_call | solution.py:310
  90.5 3.1 %copy.7 = bf16[1024,1024]{1,0:T(8,128)(2,1)} copy(bf16[1024,1024]{1,0:T(8,128)(2,1)} %sublayer.1) | data formatting | bytes 4194304

commit v6 on v5

--- a/solution.py
+++ b/solution.py
@@ -267,7 +267,7 @@
     project(inner, vt_sc, inner_first, 2 * width, inner_sums, width)
     hands_o += last(1, onward_o, False)
     hands_o += last(1, onward_o2, True)
-    pieces = 4
+    pieces = 2
     size = total // pieces
     for i in range(pieces):
         for copy in outer_copies[i * 8 // pieces:(i + 1) * 8 // pieces]:

time: 93.7 us -> 91.3 us (0.974)
  the two profiles are of different devices: /device:TPU:0 before, /device:TPU:1 now
where the time goes in v6:
time: 91.3 us; the launch traced here: 91.1 us
  Pallas kernels  88 us (96%)
  local copies, waits for them, and re-layouts  3.08 us (3%)
    pallas_call x1, Pallas kernels, shards(): pl.pallas_call(sublayer_kernel, out_shape=jax.ShapeDtypeStruct((rows, wid...  88 us
    unnamed x1, local copies, waits for them, and re-layouts  3.08 us

profile of v6, /device:TPU:1, one launch (start us, length us, event | category | flops | bytes accessed | tf_op | source)
XLA Modules:
  0.0 91.1 jit_solution(3289895260545770673)
XLA Ops:
  0.0 88.0 %sublayer.1 = bf16[1024,1024]{1,0:T(8,128)(2,1)} custom-call(s32[8,10]{1,0:T(8,128)} %layout.1, s32[8]{0:T(128)} %counts.1, bf16[1024,1024]{1,0:T(8,128)(2,1)} %x_hbm.1, bf16[128,3072]{1,0:T(8,128)(2,1)} %wq_shard.1, bf16[128,1024]{1,0:T(8,128)(2,1)} %wo_shard.1), custom_call_target="tpu_custom_call" | custom-call | tf_op jit(solution)/shard_map/sublayer/pallas_call | solution.py:310
  88.0 3.1 %copy.7 = bf16[1024,1024]{1,0:T(8,128)(2,1)} copy(bf16[1024,1024]{1,0:T(8,128)(2,1)} %sublayer.1) | data formatting | bytes 4194304

commit v7 on v6

--- a/solution.py
+++ b/solution.py
@@ -199,7 +199,7 @@
     onward_q2, more = onward(0, other_q, True)
     hands_q += more
     width = x.shape[1]
-    tile = 256
+    tile = 512
     total = x.shape[0]
     blocks = total // BLOCK
 

time: 91.3 us -> 90.4 us (level)
  no operation moved by 1% of the time
where the time goes in v7:
time: 90.4 us; the launch traced here: 90.2 us
  Pallas kernels  87.1 us (96%)
  local copies, waits for them, and re-layouts  3.08 us (3%)
    pallas_call x1, Pallas kernels, shards(): pl.pallas_call(sublayer_kernel, out_shape=jax.ShapeDtypeStruct((rows, wid...  87.1 us
    unnamed x1, local copies, waits for them, and re-layouts  3.08 us

profile of v7, /device:TPU:1, one launch (start us, length us, event | category | flops | bytes accessed | tf_op | source)
XLA Modules:
  0.0 90.2 jit_solution(14331239987856369338)
XLA Ops:
  0.0 87.1 %sublayer.1 = bf16[1024,1024]{1,0:T(8,128)(2,1)} custom-call(s32[8,10]{1,0:T(8,128)} %layout.1, s32[8]{0:T(128)} %counts.1, bf16[1024,1024]{1,0:T(8,128)(2,1)} %x_hbm.1, bf16[128,3072]{1,0:T(8,128)(2,1)} %wq_shard.1, bf16[128,1024]{1,0:T(8,128)(2,1)} %wo_shard.1), custom_call_target="tpu_custom_call" | custom-call | tf_op jit(solution)/shard_map/sublayer/pallas_call | solution.py:310
  87.1 3.1 %copy.7 = bf16[1024,1024]{1,0:T(8,128)(2,1)} copy(bf16[1024,1024]{1,0:T(8,128)(2,1)} %sublayer.1) | data formatting | bytes 4194304
